TPU v7x, 128 devices: a whole 4x4x4 slice. The times are simulated.
128 devices in a mesh: band: 8 (over x, core), mesh: 16 (over y, z).
Axes of the slice: x: 4, y: 4, z: 4, core: 2. Of those that a mesh axis runs over, the one named last changes fastest.
Arguments:
- grid_vars: bfloat16 [131072, 227], P(('band', 'mesh')), may hold values from -6 to 6
- mesh_latent: bfloat16 [40960, 512], P(('band', 'mesh')), may hold values from -6 to 6
- cotangent: bfloat16 [40960, 512], P(('band', 'mesh')), may hold values from -6 to 6
- edge_grid: int32 [524288], P(('band', 'mesh')), may hold values from 0 to 131071, as said below
- edge_mesh: int32 [524288], P(('band', 'mesh')), may hold values from 0 to 40959, as said below
- w_in: bfloat16 [227, 512], replicated, may hold values from -0.375 to 0.375
- b_in: float32 [512], replicated, may hold values from -4 to 4
- w_out: bfloat16 [512, 512], replicated, may hold values from -0.25 to 0.25
- norm_gain: float32 [512], replicated, may hold values from 0.1 to 1.9
- u_grid: bfloat16 [512, 512], replicated, may hold values from -0.25 to 0.25
- u_mesh: bfloat16 [512, 512], replicated, may hold values from -0.25 to 0.25
- b_edge: float32 [512], replicated, may hold values from -4 to 4
- w_edge: bfloat16 [512, 512], replicated, may hold values from -0.25 to 0.25
- w_self: bfloat16 [512, 512], replicated, may hold values from -0.25 to 0.25
- w_agg: bfloat16 [512, 512], replicated, may hold values from -0.1875 to 0.1875
- b_node: float32 [512], replicated, may hold values from -4 to 4
- w_node_out: bfloat16 [512, 512], replicated, may hold values from -0.25 to 0.25
Outputs:
- mesh_out: bfloat16 [40960, 512], P(('band', 'mesh'))
- grad_mesh: bfloat16 [40960, 512], P(('band', 'mesh'))
- grad_edge: float32 [512, 512], replicated
- grad_ugrid: float32 [512, 512], replicated
- grad_umesh: float32 [512, 512], replicated
Inputs may be any that keep to these rules, and one draw needn't show every extreme that they name: `edge_grid`: the edges of one device (aligned blocks of 4096) have grid nodes among that device's 1024 grid nodes. `edge_mesh`: the edges of one device have mesh nodes among the 5120 mesh nodes of the device's band (the nodes of the 16 devices of that band), in nondecreasing order within the device's block. One device's edges reach at most 48 distinct mesh nodes owned by any one device (blocks of 320 mesh nodes); this most is reached in every draw.
All inputs are finite; a program needn't handle non-finite values.
Results may differ from a plain program's by a relative error of at most 0.013.
The roundings to bfloat16 on the way count: a program that leaves them out, or rounds other values in their place, can miss the bound.
Values may be sent and summed in bfloat16 or wider, within the bound.
A program may use at most 192 MiB of HBM per device.

v0:
```python
import jax
import jax.numpy as jnp
from jax import lax
from jax.sharding import PartitionSpec as P

CAP = 48


def swish(v):
    return v * jax.nn.sigmoid(v)


def swish_grad(v):
    s = jax.nn.sigmoid(v)
    return s * (1.0 + v * (1.0 - s))


def layer_norm(v, gain):
    mean = jnp.mean(v, axis=-1, keepdims=True)
    centred = v - mean
    var = jnp.mean(centred * centred, axis=-1, keepdims=True)
    return centred * lax.rsqrt(var + 1e-05) * gain


def matmul(a, b):
    return jnp.dot(a, b, preferred_element_type=jnp.float32)


def window_take(table, ranks, block):
    width = table.shape[1]
    padded = jnp.concatenate([table, jnp.zeros((block, width), table.dtype)], axis=0)
    blocks = ranks.reshape(-1, block)
    columns = jnp.arange(block, dtype=jnp.int32)[None, :]

    def one_block(rank_block):
        base = rank_block[0]
        window = lax.dynamic_slice_in_dim(padded, base, block, 0)
        onehot = ((rank_block - base)[:, None] == columns).astype(table.dtype)
        return matmul(onehot, window).astype(table.dtype)

    return lax.map(one_block, blocks).reshape(-1, width)


def window_add(values, ranks, block, rows):
    width = values.shape[1]
    blocks = ranks.reshape(-1, block)
    value_blocks = values.reshape(-1, block, width)
    columns = jnp.arange(block, dtype=jnp.int32)[None, :]

    def one_block(index, total):
        rank_block = blocks[index]
        base = rank_block[0]
        onehot = ((rank_block - base)[:, None] == columns).astype(values.dtype)
        contrib = lax.dot_general(
            onehot,
            value_blocks[index],
            (((0,), (0,)), ((), ())),
            preferred_element_type=jnp.float32,
        )
        current = lax.dynamic_slice_in_dim(total, base, block, 0)
        return lax.dynamic_update_slice_in_dim(total, current + contrib, base, 0)

    total = lax.fori_loop(
        0, blocks.shape[0], one_block, jnp.zeros((rows + block, width), jnp.float32)
    )
    return total[:rows]


def grid_take(table, local_ids, block):
    blocks = local_ids.reshape(-1, block)
    columns = jnp.arange(table.shape[0], dtype=jnp.int32)[None, :]

    def one_block(id_block):
        onehot = (id_block[:, None] == columns).astype(table.dtype)
        return matmul(onehot, table).astype(table.dtype)

    return lax.map(one_block, blocks).reshape(-1, table.shape[1])


def grid_add(values, local_ids, block, rows):
    width = values.shape[1]
    blocks = local_ids.reshape(-1, block)
    value_blocks = values.reshape(-1, block, width)
    columns = jnp.arange(rows, dtype=jnp.int32)[None, :]

    def one_block(index, total):
        onehot = (blocks[index][:, None] == columns).astype(values.dtype)
        return total + lax.dot_general(
            onehot,
            value_blocks[index],
            (((0,), (0,)), ((), ())),
            preferred_element_type=jnp.float32,
        )

    return lax.fori_loop(0, blocks.shape[0], one_block, jnp.zeros((rows, width), jnp.float32))


def shards(
    grid_vars,
    mesh_latent,
    cotangent,
    edge_grid,
    edge_mesh,
    w_in,
    b_in,
    w_out,
    norm_gain,
    u_grid,
    u_mesh,
    b_edge,
    w_edge,
    w_self,
    w_agg,
    b_node,
    w_node_out,
):
    grid_dev = grid_vars.shape[0]
    mesh_dev = mesh_latent.shape[0]
    edge_dev = edge_grid.shape[0]
    width = mesh_latent.shape[1]
    owners = lax.axis_size("mesh")
    band_rows_count = owners * mesh_dev
    compact = owners * CAP
    block = min(512, edge_dev)
    device = lax.axis_index("band") * owners + lax.axis_index("mesh")
    grid_local = edge_grid - device * grid_dev
    mesh_local = edge_mesh - lax.axis_index("band") * band_rows_count
    fresh = jnp.concatenate(
        [jnp.ones((1,), jnp.int32), (mesh_local[1:] != mesh_local[:-1]).astype(jnp.int32)]
    )
    rank = jnp.cumsum(fresh) - 1
    node_of = jnp.full((compact,), band_rows_count, jnp.int32).at[rank].min(mesh_local, mode="drop")
    hidden = swish(matmul(grid_vars, w_in) + b_in).astype(jnp.bfloat16)
    latent = layer_norm(matmul(hidden, w_out), norm_gain).astype(jnp.bfloat16)
    proj_grid = matmul(latent, u_grid).astype(jnp.bfloat16)
    proj_mesh = matmul(mesh_latent, u_mesh).astype(jnp.bfloat16)
    edge_pgrid = grid_take(proj_grid, grid_local, block)
    owner = mesh_local // mesh_dev
    owner_ids = jnp.arange(owners, dtype=jnp.int32)[:, None]
    starts = jnp.sum(jnp.where(owner[None, :] < owner_ids, fresh[None, :], 0), axis=1)
    first = jnp.sum(jnp.where(owner[None, :] == owner_ids, starts[:, None], 0), axis=0)
    slot = owner * CAP + rank - first
    slot_of = jnp.full((compact,), compact, jnp.int32).at[rank].min(slot, mode="drop")
    ids = jnp.zeros((compact,), jnp.int32).at[slot_of].add(node_of % mesh_dev, mode="drop")
    incoming = lax.all_to_all(
        ids.reshape(owners, CAP), "mesh", split_axis=0, concat_axis=0, tiled=True
    ).reshape(-1)
    asked = proj_mesh[incoming].reshape(owners, CAP, width)
    answered = lax.all_to_all(asked, "mesh", split_axis=0, concat_axis=0, tiled=True).reshape(
        compact, width
    )
    compact_pmesh = answered.at[slot_of].get(mode="fill", fill_value=0)
    edge_pmesh = window_take(compact_pmesh, rank, block)
    pre = edge_pgrid.astype(jnp.float32) + edge_pmesh.astype(jnp.float32) + b_edge
    act = swish(pre).astype(jnp.bfloat16)
    message = matmul(act, w_edge).astype(jnp.bfloat16)
    compact_sums = window_add(message, rank, block, compact)
    partial_value = (
        jnp.zeros((compact, width), jnp.float32).at[slot_of].add(compact_sums, mode="drop")
    )
    received = lax.all_to_all(
        partial_value.reshape(owners, CAP, width), "mesh", split_axis=0, concat_axis=0, tiled=True
    ).reshape(compact, width)
    agg = jax.ops.segment_sum(received, incoming, num_segments=mesh_dev)
    agg = agg.astype(jnp.bfloat16)
    node_pre = matmul(mesh_latent, w_self) + matmul(agg, w_agg) + b_node
    node_act = swish(node_pre).astype(jnp.bfloat16)
    mesh_out = (mesh_latent.astype(jnp.float32) + matmul(node_act, w_node_out)).astype(jnp.bfloat16)
    g_node = (matmul(cotangent, w_node_out.T) * swish_grad(node_pre)).astype(jnp.bfloat16)
    g_agg = matmul(g_node, w_agg.T).astype(jnp.bfloat16)
    grad_asked = g_agg[incoming].reshape(owners, CAP, width)
    grad_answered = lax.all_to_all(
        grad_asked, "mesh", split_axis=0, concat_axis=0, tiled=True
    ).reshape(compact, width)
    compact_grads = grad_answered.at[slot_of].get(mode="fill", fill_value=0)
    g_msg = window_take(compact_grads, rank, block)
    local_edge = matmul(act.T, g_msg)
    g_edge = (matmul(g_msg, w_edge.T) * swish_grad(pre)).astype(jnp.bfloat16)
    g_pgrid = grid_add(g_edge, grid_local, block, grid_dev).astype(jnp.bfloat16)
    compact_gsums = window_add(g_edge, rank, block, compact)
    grad_partial = (
        jnp.zeros((compact, width), jnp.float32).at[slot_of].add(compact_gsums, mode="drop")
    )
    grad_received = lax.all_to_all(
        grad_partial.reshape(owners, CAP, width), "mesh", split_axis=0, concat_axis=0, tiled=True
    ).reshape(compact, width)
    g_pmesh = jax.ops.segment_sum(grad_received, incoming, num_segments=mesh_dev)
    g_pmesh = g_pmesh.astype(jnp.bfloat16)
    local_ugrid = matmul(latent.T, g_pgrid)
    local_umesh = matmul(mesh_latent.T, g_pmesh)
    summed_edge, summed_ugrid, summed_umesh = lax.psum(
        (local_edge, local_ugrid, local_umesh), ("band", "mesh")
    )
    scale = (edge_dev * lax.axis_size("band") * owners) ** (-0.5)
    grad_mesh = (
        cotangent.astype(jnp.float32) + matmul(g_node, w_self.T) + matmul(g_pmesh, u_mesh.T)
    ).astype(jnp.bfloat16)
    return (mesh_out, grad_mesh, summed_edge * scale, summed_ugrid * scale, summed_umesh * scale)


def solution(mesh):
    return jax.shard_map(
        shards,
        mesh=mesh,
        in_specs=(
            P(("band", "mesh"), None),
            P(("band", "mesh"), None),
            P(("band", "mesh"), None),
            P(("band", "mesh")),
            P(("band", "mesh")),
            P(),
            P(),
            P(),
            P(),
            P(),
            P(),
            P(),
            P(),
            P(),
            P(),
            P(),
            P(),
        ),
        out_specs=(P(("band", "mesh"), None), P(("band", "mesh"), None), P(), P(), P()),
        check_vma=False,
    )
```

profile of v0, /device:TPU:1, one launch (start us, length us, event | category | flops | bytes accessed | tf_op | source)
XLA Modules:
  0.0 675.7 jit_solution(7339228304649775887)
XLA Ops:
  9.1 28.8 %scatter_custom_fusion.1 = s32[768]{0:T(1024)S(1)} fusion(s32[4096]{0:T(1024)S(1)} %bitcast.139, s32[4096]{0:T(1024)S(1)} %get-tuple-element.495, s32[]{:T(128)} %constant.173.clone.1), kind=kCustom, calls=%fused_computation.147 | custom fusion | flops 4096 | bytes 3076 | tf_op jit(solution)/shard_map/scatter-min | solution.py:132
  37.9 28.8 %scatter_custom_fusion = s32[768]{0:T(1024)S(1)} fusion(s32[4096]{0:T(1024)S(1)} %bitcast.140, s32[4096]{0:T(1024)S(1)} %get-tuple-element.492, s32[]{:T(128)} %constant.169.clone.1), kind=kCustom, calls=%fused_computation.149 | custom fusion | flops 4096 | bytes 3076 | tf_op jit(solution)/shard_map/scatter-min | solution.py:143
  66.7 5.9 scatter_custom_fusion.2
  73.3 8.6 %all-to-all-start = ((s32[16,1,48]{2,1,0:T(1,128)}), s32[16,1,48]{2,1,0:T(1,128)S(1)}, u32[]{:S(2)}, u32[]{:S(2)}) async-start(s32[16,1,48]{2,1,0:T(1,128)} %all_to_all.18), calls=%async_computation | async-start | bytes 16384 | tf_op jit(solution)/shard_map/all_to_all | solution.py:145
  93.0 7.0 %all-to-all-start.1 = ((bf16[16,48,512]{2,1,0:T(8,128)(2,1)}), bf16[16,48,512]{2,1,0:T(8,128)(2,1)S(1)}, u32[]{:S(2)}, u32[]{:S(2)}) async-start(bf16[16,48,512]{2,1,0:T(8,128)(2,1)} %bitcast.6), calls=%async_computation.1 | async-start | bytes 1572864 | tf_op jit(solution)/shard_map/all_to_all | solution.py:149
  102.3 12.6 %while.75 = (s32[]{:T(128)}, bf16[8,512,512]{2,1,0:T(8,128)(2,1)}, s32[8,512]{1,0:T(8,128)S(1)}, bf16[1024,512]{1,0:T(8,128)(2,1)S(1)}, s32[]{:T(128)}) while((s32[]{:T(128)}, bf16[8,512,512]{2,1,0:T(8,128)(2,1)}, s32[8,512]{1,0:T(8,128)S(1)}, bf16[1024,512]{1,0:T(8,128)(2,1)S(1)}, s32[]{:T(128)}) %tuple.169), condition=%wide.region_10.11_spmd.clone, body=%wide.region_9.10_spmd.clone.sunk | while | flops 537657344 | bytes 1579585 | solution.py:77
  120.4 35.4 %while.76 = (s32[]{:T(128)}, bf16[8,512,512]{2,1,0:T(8,128)(2,1)}, s32[8,512]{1,0:T(8,128)S(1)}, bf16[1280,512]{1,0:T(8,128)(2,1)S(1)}, s32[]{:T(128)}, /*index=5*/s32[]{:T(128)}, s32[]{:T(128)}) while((s32[]{:T(128)}, bf16[8,512,512]{2,1,0:T(8,128)(2,1)}, s32[8,512]{1,0:T(8,128)S(1)}, bf16[1280,512]{1,0:T(8,128)(2,1)S(1)}, ...), condition=%wide.region_12.13_spmd.clone, body=%wide.region_11.12_spmd.clone.sunk | while | flops 268960256 | bytes 1055367 | solution.py:41
  155.8 4.8 convert_add_fusion
  164.1 4.3 convolution_convert_fusion.2
  170.2 73.9 %while.77 = (s32[]{:T(128)}, f32[1280,512]{1,0:T(8,128)}, s32[8,512]{1,0:T(8,128)S(1)}, bf16[8,512,512]{2,1,0:T(8,128)(2,1)}, s32[]{:T(128)}, /*index=5*/s32[]{:T(128)}, s32[]{:T(128)}) while((s32[]{:T(128)}, f32[1280,512]{1,0:T(8,128)}, s32[8,512]{1,0:T(8,128)S(1)}, bf16[8,512,512]{2,1,0:T(8,128)(2,1)}, s32[]{:T(128)}, ...), condition=%wide.region_14.15_spmd.clone, body=%wide.region_13.14_spmd.clone.sunk | while | flops 268960256 | bytes 4725387 | solution.py:63
  175.3 4.2 dynamic_update_slice.39
  193.8 4.1 dynamic_update_slice.39
  212.3 4.2 dynamic_update_slice.39
  244.1 8.6 %scatter_custom_fusion.3 = f32[768,512]{1,0:T(8,128)} fusion(s32[768]{0:T(1024)S(1)} %get-tuple-element.500, f32[1280,512]{1,0:T(8,128)} %get-tuple-element.370, f32[]{:T(128)} %constant.167.clone.1), kind=kCustom, calls=%fused_computation.79 | custom fusion | flops 393216 | bytes 3146240 | tf_op jit(solution)/shard_map/scatter-add | solution.py:159
  252.7 7.1 %all-to-all-start.2 = ((f32[16,48,512]{2,1,0:T(8,128)}), f32[16,48,512]{2,1,0:T(8,128)}, u32[]{:S(2)}, u32[]{:S(2)}) async-start(f32[16,48,512]{2,1,0:T(8,128)} %bitcast.10), calls=%async_computation.2 | async-start | bytes 3145728 | tf_op jit(solution)/shard_map/all_to_all | solution.py:161
  261.5 18.9 %all-to-all-done.2 = f32[16,48,512]{2,1,0:T(8,128)} async-done(((f32[16,48,512]{2,1,0:T(8,128)}), f32[16,48,512]{2,1,0:T(8,128)}, u32[]{:S(2)}, u32[]{:S(2)}) %all-to-all-start.2) | async-done | bytes 1572896 | tf_op jit(solution)/shard_map/all_to_all | solution.py:161
  280.4 7.5 %scatter_custom_fusion.4 = f32[320,512]{1,0:T(8,128)S(1)} fusion(s32[768]{0:T(1024)S(1)} %reshape.308, f32[768,512]{1,0:T(8,128)} %bitcast.11, f32[]{:T(128)} %constant.167.clone.1), kind=kCustom, calls=%fused_computation.113 | custom fusion | flops 393216 | bytes 655872 | tf_op jit(solution)/shard_map/scatter-add | solution.py:164
  293.4 4.6 all-to-all-start.3
  298.0 10.9 %all-to-all-done.3 = bf16[16,48,512]{2,1,0:T(8,128)(2,1)S(1)} async-done(((bf16[16,48,512]{2,1,0:T(8,128)(2,1)}), bf16[16,48,512]{2,1,0:T(8,128)(2,1)S(1)}, u32[]{:S(2)}, u32[]{:S(2)}) %all-to-all-start.3) | async-done | bytes 786464 | tf_op jit(solution)/shard_map/all_to_all | solution.py:172
  317.1 43.8 %while.78 = (s32[]{:T(128)}, bf16[8,512,512]{2,1,0:T(8,128)(2,1)}, s32[8,512]{1,0:T(8,128)S(1)}, bf16[1280,512]{1,0:T(8,128)(2,1)}, s32[]{:T(128)}, /*index=5*/s32[]{:T(128)}, s32[]{:T(128)}) while((s32[]{:T(128)}, bf16[8,512,512]{2,1,0:T(8,128)(2,1)}, s32[8,512]{1,0:T(8,128)S(1)}, bf16[1280,512]{1,0:T(8,128)(2,1)}, s32[]{:T(128)}, ...), condition=%wide.region_18.19_spmd.clone, body=%wide.region_17.18_spmd.clone.sunk | while | flops 268960256 | bytes 1055367 | solution.py:41
  360.9 8.4 %multiply_convert_fusion.1 = bf16[4096,512]{1,0:T(8,128)(2,1)} fusion(f32[8,512,512]{2,1,0:T(8,128)} %copy-done.2, bf16[4096,512]{1,0:T(8,128)(2,1)} %bitcast.127, bf16[512,512]{1,0:T(8,128)(2,1)S(1)} %copy-done, f32[512]{0:T(512)S(1)} %copy-done.21), kind=kOutput, calls=%fused_computation.68 | convolution fusion | flops 2168455168 | bytes 17303552 | tf_op jit(solution)/shard_map/dot_general | solution.py:26
  369.2 18.9 %while.80 = (s32[]{:T(128)}, f32[1024,512]{1,0:T(8,128)S(1)}, s32[8,512]{1,0:T(8,128)S(1)}, bf16[8,512,512]{2,1,0:T(8,128)(2,1)}, s32[]{:T(128)}, /*index=5*/s32[]{:T(128)}) while((s32[]{:T(128)}, f32[1024,512]{1,0:T(8,128)S(1)}, s32[8,512]{1,0:T(8,128)S(1)}, bf16[8,512,512]{2,1,0:T(8,128)(2,1)}, s32[]{:T(128)}, ...), condition=%wide.region_25.26_spmd.clone, body=%wide.region_24.25_spmd.clone.sunk | while | flops 538443776 | bytes 4725331 | solution.py:95
  393.3 73.8 %while.79 = (s32[]{:T(128)}, f32[1280,512]{1,0:T(8,128)}, s32[8,512]{1,0:T(8,128)S(1)}, bf16[8,512,512]{2,1,0:T(8,128)(2,1)}, s32[]{:T(128)}, /*index=5*/s32[]{:T(128)}, s32[]{:T(128)}) while((s32[]{:T(128)}, f32[1280,512]{1,0:T(8,128)}, s32[8,512]{1,0:T(8,128)S(1)}, bf16[8,512,512]{2,1,0:T(8,128)(2,1)}, s32[]{:T(128)}, ...), condition=%wide.region_20.21_spmd.clone, body=%wide.region_19.20_spmd.clone.sunk | while | flops 268960256 | bytes 4725387 | solution.py:63
  398.4 4.1 dynamic_update_slice.41
  416.9 4.1 dynamic_update_slice.41
  435.4 4.1 dynamic_update_slice.41
  463.0 4.1 dynamic_update_slice.41
  467.2 8.6 %scatter_custom_fusion.5 = f32[768,512]{1,0:T(8,128)} fusion(s32[768]{0:T(1024)S(1)} %get-tuple-element.500, f32[1280,512]{1,0:T(8,128)} %get-tuple-element.372, f32[]{:T(128)} %constant.167.clone.1), kind=kCustom, calls=%fused_computation.77 | custom fusion | flops 393216 | bytes 3146240 | tf_op jit(solution)/shard_map/scatter-add | solution.py:182
  479.8 8.8 %fusion.45 = f32[512,512]{1,0:T(8,128)} fusion(bf16[8,512,512]{2,1,0:T(8,128)(2,1)} %get-tuple-element.371, f32[512]{0:T(512)S(1)} %copy-done.21, bf16[8,512,512]{2,1,0:T(8,128)(2,1)} %get-tuple-element.369, bf16[8,512,512]{2,1,0:T(8,128)(2,1)} %get-tuple-element.368), kind=kOutput, calls=%fused_computation.83 | convolution fusion | flops 2166358016 | bytes 13633536 | tf_op jit(solution)/shard_map/dot_general | solution.py:26
  488.6 9.9 %all-to-all-done.4 = f32[16,48,512]{2,1,0:T(8,128)S(1)} async-done(((f32[16,48,512]{2,1,0:T(8,128)}), f32[16,48,512]{2,1,0:T(8,128)S(1)}, u32[]{:S(2)}, u32[]{:S(2)}) %all-to-all-start.4) | async-done | bytes 1572896 | tf_op jit(solution)/shard_map/all_to_all | solution.py:184
  498.4 6.9 %scatter_custom_fusion.6 = f32[320,512]{1,0:T(8,128)S(1)} fusion(s32[768]{0:T(1024)S(1)} %reshape.308, f32[768,512]{1,0:T(8,128)S(1)} %bitcast.129, f32[]{:T(128)} %constant.167.clone.1), kind=kCustom, calls=%fused_computation.111 | custom fusion | flops 393216 | bytes 655364 | tf_op jit(solution)/shard_map/scatter-add | solution.py:187
  510.2 153.6 %all-reduce.5.cloned.1.call-done = (f32[512,512]{1,0:T(8,128)}, f32[512,512]{1,0:T(8,128)}, f32[512,512]{1,0:T(8,128)}) async-done(((f32[512,512]{1,0:T(8,128)}, f32[512,512]{1,0:T(8,128)}, f32[512,512]{1,0:T(8,128)}), (f32[512,512]{1,0:T(8,128)}, f32[512,512]{1,0:T(8,128)}, f32[512,512]{1,0:T(8,128)})) %all-reduce.5.cloned.1.call-update) | async-done | bytes 3145744 | tf_op jit(solution)/shard_map/psum | solution.py:191
  (253 shorter events, 227.0 us)
Async XLA Ops:
  7.2 156.9 %copy-start = (bf16[512,512]{1,0:T(8,128)(2,1)S(1)}, bf16[512,512]{1,0:T(8,128)(2,1)}, u32[]{:S(2)}) copy-start(bf16[512,512]{1,0:T(8,128)(2,1)} %param.41) | copy-start | bytes 1572868
  73.3 16.3 %all-to-all-start = ((s32[16,1,48]{2,1,0:T(1,128)}), s32[16,1,48]{2,1,0:T(1,128)S(1)}, u32[]{:S(2)}, u32[]{:S(2)}) async-start(s32[16,1,48]{2,1,0:T(1,128)} %all_to_all.18), calls=%async_computation | async-start | bytes 16384 | tf_op jit(solution)/shard_map/all_to_all | solution.py:145
  81.9 3.0 copy-start.4
  84.5 5.0 copy-start.3
  84.5 2.1 copy-start.19
  84.8 4.7 copy-start.18
  93.0 9.3 %copy-start.24 = (bf16[1024,512]{1,0:T(8,128)(2,1)S(1)}, bf16[1024,512]{1,0:T(8,128)(2,1)}, u32[]{:S(2)}) copy-start(bf16[1024,512]{1,0:T(8,128)(2,1)} %convolution_convert_fusion.3) | copy-start | bytes 3145732
  93.0 22.1 %all-to-all-start.1 = ((bf16[16,48,512]{2,1,0:T(8,128)(2,1)}), bf16[16,48,512]{2,1,0:T(8,128)(2,1)S(1)}, u32[]{:S(2)}, u32[]{:S(2)}) async-start(bf16[16,48,512]{2,1,0:T(8,128)(2,1)} %bitcast.6), calls=%async_computation.1 | async-start | bytes 1572864 | tf_op jit(solution)/shard_map/all_to_all | solution.py:149
  155.8 4.8 copy-start.21
  160.6 3.4 copy-start.2
  244.1 15.8 %copy-start.6 = (bf16[512,512]{1,0:T(8,128)(2,1)S(1)}, bf16[512,512]{1,0:T(8,128)(2,1)}, u32[]{:S(2)}) copy-start(bf16[512,512]{1,0:T(8,128)(2,1)} %param.42) | copy-start | bytes 1572868
  252.7 35.2 %copy-start.8 = (bf16[512,512]{1,0:T(8,128)(2,1)S(1)}, bf16[512,512]{1,0:T(8,128)(2,1)}, u32[]{:S(2)}) copy-start(bf16[512,512]{1,0:T(8,128)(2,1)} %param.43) | copy-start | bytes 1572868
  252.7 35.3 %copy-start.20 = (f32[512]{0:T(512)S(1)}, f32[512]{0:T(512)}, u32[]{:S(2)}) copy-start(f32[512]{0:T(512)} %param.44) | copy-start | bytes 6148
  252.7 27.7 %all-to-all-start.2 = ((f32[16,48,512]{2,1,0:T(8,128)}), f32[16,48,512]{2,1,0:T(8,128)}, u32[]{:S(2)}, u32[]{:S(2)}) async-start(f32[16,48,512]{2,1,0:T(8,128)} %bitcast.10), calls=%async_computation.2 | async-start | bytes 3145728 | tf_op jit(solution)/shard_map/all_to_all | solution.py:161
  259.9 29.3 %copy-start.16 = (bf16[320,512]{1,0:T(8,128)(2,1)S(1)}, bf16[320,512]{1,0:T(8,128)(2,1)}, u32[]{:S(2)}) copy-start(bf16[320,512]{1,0:T(8,128)(2,1)} %param.31) | copy-start | bytes 983044
  260.2 29.0 %copy-start.22 = (bf16[512,512]{1,0:T(8,128)(2,1)S(1)}, bf16[512,512]{1,0:T(8,128)(2,1)}, u32[]{:S(2)}) copy-start(bf16[512,512]{1,0:T(8,128)(2,1)} %param.45) | copy-start | bytes 1572868
  288.3 0.9 copy-start.14
  289.6 3.7 copy-start.10
  293.4 15.5 %all-to-all-start.3 = ((bf16[16,48,512]{2,1,0:T(8,128)(2,1)}), bf16[16,48,512]{2,1,0:T(8,128)(2,1)S(1)}, u32[]{:S(2)}, u32[]{:S(2)}) async-start(bf16[16,48,512]{2,1,0:T(8,128)(2,1)} %bitcast.12), calls=%async_computation.3 | async-start | bytes 1572864 | tf_op jit(solution)/shard_map/all_to_all | solution.py:172
  475.7 22.7 %all-to-all-start.4 = ((f32[16,48,512]{2,1,0:T(8,128)}), f32[16,48,512]{2,1,0:T(8,128)S(1)}, u32[]{:S(2)}, u32[]{:S(2)}) async-start(f32[16,48,512]{2,1,0:T(8,128)} %bitcast.16), calls=%async_computation.4 | async-start | bytes 3145728 | tf_op jit(solution)/shard_map/all_to_all | solution.py:184
  479.5 25.8 %copy-start.5 = (bf16[320,512]{1,0:T(8,128)(2,1)S(1)}, bf16[320,512]{1,0:T(8,128)(2,1)}, u32[]{:S(2)}) copy-start(bf16[320,512]{1,0:T(8,128)(2,1)} %param.30) | copy-start | bytes 983044
  479.5 184.3 %all-reduce.5.cloned.1.call-start = ((), (), s32[]{:S(2)}) async-start(), calls=%async_computation.5 | async-start | bytes 6291456 | tf_op jit(solution)/shard_map/psum | solution.py:191
  505.3 1.5 copy-start.7
  505.3 1.5 copy-start.11
  505.3 1.5 copy-start.17
  506.8 1.1 copy-start.15
  506.8 1.2 copy-start.23
  506.9 2.3 copy-start.9
  663.8 2.5 copy-start.13
  663.8 3.5 copy-start.12
  663.8 4.6 copy-start.1
Sparse Core Ops, SparseCore 0:
  506.9 156.8 all-reduce.4
where the time goes:
time: 686 us; the launch traced here: 676 us
  waiting for transfers between devices  193 us (28%)
  other arithmetic  133 us (19%)
  matrix products  129 us (19%)
  local copies, waits for them, and re-layouts  111 us (16%)
  loops' own time  62.9 us (9%)
  starting transfers between devices  31.3 us (5%)
  between operations  15 us (2%)
    psum x1, waiting for transfers between devices, shards(): lax.psum((local_edge, local_ugrid, local_umesh), ('band', 'mesh'))  154 us
    dot_general x39, matrix products, matmul(): return jnp.dot(a, b, preferred_element_type=jnp.float32)  79.4 us
    dynamic_update_slice x16, local copies, waits for them, and re-layouts, one_block(): return lax.dynamic_update_slice_in_dim(total, current + contrib, base, 0)  66.1 us
    dot_general x24, matrix products, one_block(): lax.dot_general(onehot, value_blocks[index], (((0,), (0,)), ((), ())), pr...  50.1 us
    another operation x2, loops' own time, window_add(): lax.fori_loop(0, blocks.shape[0], one_block, jnp.zeros((rows + block, wid...  31.4 us
    another operation x2, loops' own time, window_take(): return lax.map(one_block, blocks).reshape(-1, width)  31.2 us
    another operation x1, other arithmetic, shards(): jnp.full((compact,), band_rows_count, jnp.int32).at[rank]  28.8 us
    another operation x1, other arithmetic, shards(): jnp.full((compact,), compact, jnp.int32).at[rank].min(slot, mode='drop')  28.8 us
  transfers between devices with their start and end apart: 6, of which 4 were waited for; matrix products, arithmetic and copies ran while one was open for 5% of the time, Pallas kernels for 0%

commit v1 on v0

v1 whole, which is shorter than its diff:
```python
import functools

import jax
import jax.numpy as jnp
from jax import lax
from jax.experimental import pallas as pl
from jax.experimental.pallas import tpu as pltpu
from jax.sharding import PartitionSpec as P

CAP = 48
MESH = pl.DeviceIdType.MESH
F32 = jnp.float32
BF16 = jnp.bfloat16
VMEM_LIMIT = 60 * 1024 * 1024


def sigmoid(v):
    return 0.5 + 0.5 * jnp.tanh(0.5 * v)


def dot(a, b):
    return jnp.dot(a, b, preferred_element_type=F32)


def dot_nt(a, b):
    return lax.dot_general(a, b, (((1,), (1,)), ((), ())), preferred_element_type=F32)


def dot_tn(a, b):
    return lax.dot_general(a, b, (((0,), (0,)), ((), ())), preferred_element_type=F32)


def iota(shape, dim):
    return lax.broadcasted_iota(jnp.int32, shape, dim)


def onehot(mask):
    return jnp.where(mask, 1.0, 0.0).astype(BF16)


def enter(axes):
    barrier = pltpu.get_barrier_semaphore()
    total = 0
    for axis, n in axes:
        me = lax.axis_index(axis)
        for d in range(1, n):
            pl.semaphore_signal(
                barrier, inc=1, device_id={axis: lax.rem(me + d, n)}, device_id_type=MESH
            )
        total += n - 1
    pl.semaphore_wait(barrier, total)


def send_all(axis, n, src, dst, send_sem, recv_sem):
    me = lax.axis_index(axis)
    copies = []
    for d in range(1, n):
        peer = lax.rem(me + d, n)
        copy = pltpu.make_async_remote_copy(
            src_ref=src(peer),
            dst_ref=dst(me),
            send_sem=send_sem.at[d],
            recv_sem=recv_sem.at[d],
            device_id={axis: peer},
            device_id_type=MESH,
        )
        copy.start()
        copies.append(copy)
    return copies


def wait_all(copies):
    for copy in copies:
        copy.wait()


def columns(rows_ref, out_ref):
    rows = rows_ref.shape[0]
    values = rows_ref[...].astype(F32)
    pad = jnp.zeros((128 - rows, 128), F32)
    turned = jnp.transpose(jnp.concatenate([values, pad], axis=0))
    for r in range(rows):
        out_ref[r * 128 : (r + 1) * 128, :] = jnp.broadcast_to(
            turned[:, r : r + 1], (128, 128)
        ).astype(jnp.int32)


def fetch_kernel(
    nb, nm, em, eg, gv, ml, w_in, b_in, w_out, gain, u_grid, u_mesh,
    table, pick, latent, pgrid, slots, slot_col, grid_col,
    local_grid, left, right, ids_out, ids_in, asked, landed, pmesh, s1, r1, s2, r2,
):
    mesh_dev = ml.shape[0]
    grid_dev = gv.shape[0]
    rows = em.shape[0]
    me = lax.axis_index("mesh")
    band = lax.axis_index("band")
    enter((("mesh", nm),))
    x = em[...] - band * (nm * mesh_dev)
    lane = iota(x.shape, 1)
    row = iota(x.shape, 0)
    prev = pltpu.roll(x, 1, 1)
    prev = jnp.where(lane == 0, pltpu.roll(prev, 1, 0), prev)
    fresh = jnp.where((x != prev) | ((lane == 0) & (row == 0)), 1.0, 0.0)
    fb = fresh.astype(BF16)
    upper = onehot(iota((128, 128), 0) <= iota((128, 128), 1))
    totals = dot(fb, jnp.ones((128, 128), BF16)).astype(BF16)
    lower = onehot(iota((rows, rows), 1) < iota((rows, rows), 0))
    rank = dot(fb, upper) + dot(lower, totals) - 1.0
    owner = jnp.zeros(x.shape, jnp.int32)
    first = jnp.zeros(x.shape, F32)
    for o in range(1, nm):
        later = x >= o * mesh_dev
        begun = jnp.sum(jnp.where(later, 0.0, fresh), keepdims=True)
        owner = owner + jnp.where(later, 1, 0)
        first = jnp.where(later, begun, first)
    inner = (rank - first).astype(jnp.int32)
    slots[...] = owner * CAP + inner
    node = x - owner * mesh_dev
    high = jnp.right_shift(node, 4)
    low = node - high * 16
    high = jnp.where(fresh > 0, high, 0).astype(F32)
    low = jnp.where(fresh > 0, low, 0).astype(F32)
    owner_id = iota((nm, 128), 0)
    inner_id = iota((128, 128), 0)
    for r in range(rows):
        cut = slice(r * 128, (r + 1) * 128)
        mine = owner[r : r + 1, :] == owner_id
        left[0:nm, cut] = jnp.where(mine, high[r : r + 1, :], 0.0).astype(BF16)
        left[nm : 2 * nm, cut] = jnp.where(mine, low[r : r + 1, :], 0.0).astype(BF16)
        right[:, cut] = onehot(inner[r : r + 1, :] == inner_id)
    both = dot_nt(left[...], right[...])
    ids = both[0:nm] * 16.0 + both[nm : 2 * nm]
    for o in range(nm):
        ids_out[o] = jnp.broadcast_to(ids[o : o + 1, :], (8, 128))
    sent = send_all("mesh", nm, lambda p: ids_out.at[p], lambda q: ids_in.at[q], s1, r1)
    ids_in[me] = ids_out[me]
    pmesh[0:mesh_dev, :] = dot(ml[...], u_mesh[...]).astype(BF16)
    pmesh[mesh_dev:, :] = jnp.zeros((pmesh.shape[0] - mesh_dev, pmesh.shape[1]), BF16)
    columns(slots, slot_col)
    local_grid[...] = eg[...] - (band * nm + me) * grid_dev
    columns(local_grid, grid_col)
    wait_all(sent)
    turned = jnp.transpose(ids_in[...].reshape(nm * 8, 128))
    for q in range(nm):
        ids_q = jnp.broadcast_to(turned[0:CAP, q * 8 : q * 8 + 1], (CAP, 128)).astype(jnp.int32)
        for t in range(pick.shape[1] // 128):
            pick[q * CAP : (q + 1) * CAP, t * 128 : (t + 1) * 128] = onehot(
                ids_q == iota((CAP, 128), 1) + t * 128
            )
    asked[...] = dot(pick[...], pmesh[...]).astype(BF16).reshape(asked.shape)
    sent = send_all("mesh", nm, lambda p: asked.at[p], lambda q: landed.at[q], s2, r2)
    landed[me] = asked[me]
    step = 256

    def grid_rows(i, carry):
        cut = pl.ds(pl.multiple_of(i * step, step), step)
        v = dot(gv[cut, :], w_in[...]) + b_in[...]
        hidden = (v * sigmoid(v)).astype(BF16)
        y = dot(hidden, w_out[...])
        centred = y - jnp.mean(y, axis=-1, keepdims=True)
        var = jnp.mean(centred * centred, axis=-1, keepdims=True)
        lat = (centred * lax.rsqrt(var + 1e-05) * gain[...]).astype(BF16)
        latent[cut, :] = lat
        pgrid[cut, :] = dot(lat, u_grid[...]).astype(BF16)
        return carry

    lax.fori_loop(0, grid_dev // step, grid_rows, 0)
    wait_all(sent)
    table[...] = landed[...].reshape(table.shape)


EB = 512
TB = 256


def edge_kernel(slot_s, slots, grid_rows, slot_col, grid_col, table, pgrid, b_edge,
                a_out, s_out, slope, acc, pre, both):
    rows = slots.shape[0]
    width = table.shape[1]
    tiles = table.shape[0] // TB
    per = EB // 128
    acc[...] = jnp.zeros_like(acc)

    def block(b, carry):
        cut = pl.ds(pl.multiple_of(b * EB, EB), EB)
        gcol = grid_col[cut, :]
        hot = jnp.concatenate(
            [onehot(gcol == iota((EB, 128), 1) + t * 128) for t in range(pgrid.shape[0] // 128)],
            axis=1,
        )
        pre[...] = dot(hot, pgrid[...]) + b_edge[...]
        low = slot_s[b * per, 0]
        high = slot_s[b * per + per - 1, 127]
        for t in range(tiles):
            @pl.when((low < (t + 1) * TB) & (high >= t * TB))
            def _():
                scol = slot_col[cut, :]
                hot = jnp.concatenate(
                    [onehot(scol == iota((EB, 128), 1) + (t * TB + u * 128)) for u in range(TB // 128)],
                    axis=1,
                )
                pre[...] += dot(hot, table[t * TB : (t + 1) * TB, :])

        v = pre[...]
        s = sigmoid(v)
        act = v * s
        both[:, 0:width] = act.astype(BF16)
        sl = (s + act * (1.0 - s)).astype(BF16)
        both[:, width:] = sl
        slope[cut, :] = sl
        for t in range(tiles):
            @pl.when((low < (t + 1) * TB) & (high >= t * TB))
            def _():
                hot = jnp.concatenate(
                    [onehot(slots[pl.ds(b * per + u, 1), :] == iota((TB, 128), 0) + t * TB) for u in range(per)],
                    axis=1,
                )
                acc[t * TB : (t + 1) * TB, :] += dot(hot, both[...])

        return carry

    lax.fori_loop(0, rows // per, block, 0)
    a_out[...] = acc[:, 0:width].astype(BF16)
    s_out[...] = acc[:, width:].astype(BF16)


def node_kernel(
    nm, a_part, s_part, pick, ml, ct, w_edge, w_self, w_agg, b_node, w_node, u_mesh,
    mesh_out, grad_mesh, htable, g_edge, g_umesh,
    a_in, s_in, asked, landed, s1, r1, s2, r2, s3, r3,
):
    mesh_dev = ml.shape[0]
    me = lax.axis_index("mesh")
    enter((("mesh", nm),))
    sent_a = send_all("mesh", nm, lambda p: a_part.at[p], lambda q: a_in.at[q], s1, r1)
    sent_s = send_all("mesh", nm, lambda p: s_part.at[p], lambda q: s_in.at[q], s2, r2)
    a_in[me] = a_part[me]
    s_in[me] = s_part[me]
    flat = (a_in.shape[0] * a_in.shape[1], a_in.shape[2])
    own = dot(ml[...], w_self[...]) + b_node[...]
    back = dot_nt(ct[...], w_node[...])
    wait_all(sent_a)
    acts = dot_tn(pick[...], a_in[...].reshape(flat))[0:mesh_dev].astype(BF16)
    agg = dot(acts, w_edge[...]).astype(BF16)
    node_pre = own + dot(agg, w_agg[...])
    s = sigmoid(node_pre)
    node_act = node_pre * s
    g_node = (back * (s + node_act * (1.0 - s))).astype(BF16)
    g_agg = dot_nt(g_node, w_agg[...]).astype(BF16)
    h = dot_nt(g_agg, w_edge[...])
    hb = jnp.concatenate(
        [h.astype(BF16), jnp.zeros((pick.shape[1] - mesh_dev, h.shape[1]), BF16)], axis=0
    )
    asked[...] = dot(pick[...], hb).astype(BF16).reshape(asked.shape)
    sent_h = send_all("mesh", nm, lambda p: asked.at[p], lambda q: landed.at[q], s3, r3)
    landed[me] = asked[me]
    mesh_out[...] = (ml[...].astype(F32) + dot(node_act.astype(BF16), w_node[...])).astype(BF16)
    g_edge[...] = dot_tn(acts, g_agg).astype(BF16)
    part = ct[...].astype(F32) + dot_nt(g_node, w_self[...])
    wait_all(sent_s)
    slopes = dot_tn(pick[...], s_in[...].reshape(flat))[0:mesh_dev]
    g_pmesh = (h * slopes).astype(BF16)
    g_umesh[...] = dot_tn(ml[...], g_pmesh).astype(BF16)
    grad_mesh[...] = (part + dot_nt(g_pmesh, u_mesh[...])).astype(BF16)
    wait_all(sent_h)
    htable[...] = landed[...].reshape(htable.shape)


def grid_kernel(slot_s, grid_rows, slot_col, htable, slope, latent, g_ugrid, acc, pre):
    rows = grid_rows.shape[0]
    tiles = htable.shape[0] // TB
    per = EB // 128
    acc[...] = jnp.zeros_like(acc)

    def block(b, carry):
        cut = pl.ds(pl.multiple_of(b * EB, EB), EB)
        low = slot_s[b * per, 0]
        high = slot_s[b * per + per - 1, 127]
        pre[...] = jnp.zeros_like(pre)
        for t in range(tiles):
            @pl.when((low < (t + 1) * TB) & (high >= t * TB))
            def _():
                scol = slot_col[cut, :]
                hot = jnp.concatenate(
                    [onehot(scol == iota((EB, 128), 1) + (t * TB + u * 128)) for u in range(TB // 128)],
                    axis=1,
                )
                pre[...] += dot(hot, htable[t * TB : (t + 1) * TB, :])

        g = (pre[...] * slope[cut, :].astype(F32)).astype(BF16)
        n = acc.shape[0]
        hot = jnp.concatenate(
            [onehot(grid_rows[pl.ds(b * per + u, 1), :] == iota((n, 128), 0)) for u in range(per)],
            axis=1,
        )
        acc[...] += dot(hot, g)
        return carry

    lax.fori_loop(0, rows // per, block, 0)
    g_ugrid[...] = dot_tn(latent[...], acc[...].astype(BF16)).astype(BF16)


def reduce_kernel(nb, nm, scale, ge, gu, gg, oe, ou, og, *scratch):
    axes = {"band": nb, "mesh": nm}
    enter((("band", nb), ("mesh", nm)))
    width = ge.shape[1]
    plans = []
    for i, (src, out) in enumerate(((ge, oe), (gu, ou), (gg, og))):
        big, small = ("mesh", "band") if i == 2 else ("band", "mesh")
        plans.append((src, out, big, small) + tuple(scratch[i * 10 : (i + 1) * 10]))
    stage = []
    for src, out, big, small, in1, mid, in2, own, all2, all1, *sems in plans:
        n = axes[big]
        rows = in1.shape[1]
        stage.append(send_all(
            big, n,
            lambda p, src=src, rows=rows: src.at[pl.ds(pl.multiple_of(p * rows, 16), rows), :],
            lambda q, in1=in1: in1.at[q], sems[0].at[0], sems[0].at[1]))
        me = lax.axis_index(big)
        in1[me] = src[pl.ds(pl.multiple_of(me * rows, 16), rows), :]
    nxt = []
    for k, (src, out, big, small, in1, mid, in2, own, all2, all1, *sems) in enumerate(plans):
        wait_all(stage[k])
        n, m = axes[big], axes[small]
        total = in1[0].astype(F32)
        for q in range(1, n):
            total = total + in1[q].astype(F32)
        total = total.astype(BF16)
        pr, pc = mid.shape[1], mid.shape[2]
        cols = width // pc
        for i in range(m):
            a, c = i // cols, i % cols
            mid[i] = total[a * pr : (a + 1) * pr, c * pc : (c + 1) * pc]
        nxt.append(send_all(small, m, lambda p, mid=mid: mid.at[p], lambda q, in2=in2: in2.at[q],
                            sems[1].at[0], sems[1].at[1]))
        me = lax.axis_index(small)
        in2[me] = mid[me]
    stage, nxt = nxt, []
    for k, (src, out, big, small, in1, mid, in2, own, all2, all1, *sems) in enumerate(plans):
        wait_all(stage[k])
        m = axes[small]
        total = in2[0].astype(F32)
        for q in range(1, m):
            total = total + in2[q].astype(F32)
        own[...] = (total * scale).astype(BF16)
        nxt.append(send_all(small, m, lambda p, own=own: own, lambda q, all2=all2: all2.at[q],
                            sems[2].at[0], sems[2].at[1]))
        all2[lax.axis_index(small)] = own[...]
    stage, nxt = nxt, []
    for k, (src, out, big, small, in1, mid, in2, own, all2, all1, *sems) in enumerate(plans):
        wait_all(stage[k])
        n, m = axes[big], axes[small]
        pr, pc = mid.shape[1], mid.shape[2]
        cols = width // pc
        me = lax.axis_index(big)
        for i in range(m):
            a, c = i // cols, i % cols
            all1[me, a * pr : (a + 1) * pr, c * pc : (c + 1) * pc] = all2[i]
        nxt.append(send_all(big, n, lambda p, all1=all1, me=me: all1.at[me], lambda q, all1=all1: all1.at[q],
                            sems[3].at[0], sems[3].at[1]))
    for k, (src, out, big, small, in1, mid, in2, own, all2, all1, *sems) in enumerate(plans):
        wait_all(nxt[k])
        out[...] = all1[...].reshape(out.shape).astype(F32)


def vmem():
    return pl.BlockSpec(memory_space=pltpu.VMEM)


def shape(dims, kind):
    return jax.ShapeDtypeStruct(dims, kind)


def params(cid=None):
    if cid is None:
        return pltpu.CompilerParams(vmem_limit_bytes=VMEM_LIMIT)
    return pltpu.CompilerParams(
        vmem_limit_bytes=VMEM_LIMIT, collective_id=cid, has_side_effects=True
    )


def shards(
    nb, nm, grid_vars, mesh_latent, cotangent, edge_grid, edge_mesh, w_in, b_in, w_out, norm_gain,
    u_grid, u_mesh, b_edge, w_edge, w_self, w_agg, b_node, w_node_out,
):
    grid_dev = grid_vars.shape[0]
    mesh_dev, width = mesh_latent.shape
    edges = edge_grid.shape[0]
    rows = edges // 128
    slots_n = nm * CAP
    padded = -(-mesh_dev // 128) * 128
    sem = pltpu.SemaphoreType.DMA
    em = edge_mesh.reshape(rows, 128)
    eg = edge_grid.reshape(rows, 128)
    table, pick, latent, pgrid, slots, slot_col, grid_col, local_grid = pl.pallas_call(
        functools.partial(fetch_kernel, nb, nm),
        out_shape=(
            shape((slots_n, width), BF16), shape((slots_n, padded), BF16),
            shape((grid_dev, width), BF16), shape((grid_dev, width), BF16),
            shape((rows, 128), jnp.int32), shape((edges, 128), jnp.int32),
            shape((edges, 128), jnp.int32), shape((rows, 128), jnp.int32),
        ),
        in_specs=[vmem()] * 10,
        out_specs=(vmem(),) * 8,
        scratch_shapes=[
            pltpu.VMEM((2 * nm, edges), BF16), pltpu.VMEM((128, edges), BF16),
            pltpu.VMEM((nm, 8, 128), F32), pltpu.VMEM((nm, 8, 128), F32),
            pltpu.VMEM((nm, CAP, width), BF16), pltpu.VMEM((nm, CAP, width), BF16),
            pltpu.VMEM((padded, width), BF16),
            sem((nm,)), sem((nm,)), sem((nm,)), sem((nm,)),
        ],
        compiler_params=params(0),
        name="fetch",
    )(em, eg, grid_vars, mesh_latent, w_in, b_in.reshape(1, -1), w_out, norm_gain.reshape(1, -1),
      u_grid, u_mesh)
    a_part, s_part, slope = pl.pallas_call(
        edge_kernel,
        out_shape=(shape((slots_n, width), BF16), shape((slots_n, width), BF16), shape((edges, width), BF16)),
        in_specs=[pl.BlockSpec(memory_space=pltpu.SMEM)] + [vmem()] * 7,
        out_specs=(vmem(),) * 3,
        scratch_shapes=[
            pltpu.VMEM((slots_n, 2 * width), F32), pltpu.VMEM((EB, width), F32),
            pltpu.VMEM((EB, 2 * width), BF16),
        ],
        compiler_params=params(),
        name="edges",
    )(slots, slots, local_grid, slot_col, grid_col, table, pgrid, b_edge.reshape(1, -1))
    mesh_out, grad_mesh, htable, g_edge, g_umesh = pl.pallas_call(
        functools.partial(node_kernel, nm),
        out_shape=(
            shape((mesh_dev, width), BF16), shape((mesh_dev, width), BF16), shape((slots_n, width), BF16),
            shape((width, width), BF16), shape((width, width), BF16),
        ),
        in_specs=[vmem()] * 11,
        out_specs=(vmem(),) * 5,
        scratch_shapes=[pltpu.VMEM((nm, CAP, width), BF16)] * 4 + [sem((nm,))] * 6,
        compiler_params=params(1),
        name="nodes",
    )(a_part.reshape(nm, CAP, width), s_part.reshape(nm, CAP, width), pick, mesh_latent, cotangent,
      w_edge, w_self, w_agg, b_node.reshape(1, -1), w_node_out, u_mesh)
    g_ugrid = pl.pallas_call(
        grid_kernel,
        out_shape=shape((width, width), BF16),
        in_specs=[pl.BlockSpec(memory_space=pltpu.SMEM)] + [vmem()] * 5,
        out_specs=vmem(),
        scratch_shapes=[pltpu.VMEM((grid_dev, width), F32), pltpu.VMEM((EB, width), F32)],
        compiler_params=params(),
        name="grids",
    )(slots, local_grid, slot_col, htable, slope, latent)
    scratch = []
    for i in range(3):
        n, m = (nm, nb) if i == 2 else (nb, nm)
        big = width // n
        pc = min(4, m)
        piece = (big // (m // pc), width // pc)
        scratch += [
            pltpu.VMEM((n, big, width), BF16), pltpu.VMEM((m,) + piece, BF16),
            pltpu.VMEM((m,) + piece, BF16), pltpu.VMEM(piece, BF16), pltpu.VMEM((m,) + piece, BF16),
            pltpu.VMEM((n, big, width), BF16),
            sem((2, n)), sem((2, m)), sem((2, m)), sem((2, n)),
        ]
    scale = (edges * nb * nm) ** (-0.5)
    out = shape((width, width), F32)
    grad_edge, grad_umesh, grad_ugrid = pl.pallas_call(
        functools.partial(reduce_kernel, nb, nm, scale),
        out_shape=(out, out, out),
        in_specs=[vmem()] * 3,
        out_specs=(vmem(),) * 3,
        scratch_shapes=scratch,
        compiler_params=params(2),
        name="reduce",
    )(g_edge, g_umesh, g_ugrid)
    return (mesh_out, grad_mesh, grad_edge, grad_ugrid, grad_umesh)


def solution(mesh):
    split = P(("band", "mesh"), None)
    flat = P(("band", "mesh"))
    return jax.shard_map(
        functools.partial(shards, mesh.shape["band"], mesh.shape["mesh"]),
        mesh=mesh,
        in_specs=(split, split, split, flat, flat) + (P(),) * 12,
        out_specs=(split, split, P(), P(), P()),
        check_vma=False,
    )
```

time: 686 us -> 154 us (0.22); the launches traced: 676 us -> 154 us
  waiting for transfers between devices: 193 us -> 0 us
  Pallas kernels: 0 us -> 145 us
  other arithmetic: 133 us -> 0 us
  matrix products: 129 us -> 0 us
  local copies, waits for them, and re-layouts: 111 us -> 7.78 us
  loops' own time: 62.9 us -> 0 us
  starting transfers between devices: 31.3 us -> 0 us
  between operations: 15 us -> 0.68 us
    psum x1 -> x0, waiting for transfers between devices: 154 us -> none  [shards(): lax.psum((local_edge, local_ugrid, local_umesh), ('band', 'mesh'))]
    pallas_call x0 -> x5, Pallas kernels: none -> 145 us  [the longest x1 48 us: shards(): pl.pallas_call(functools.partial(reduce_kernel, nb, nm, scale), out_shape...]
    dot_general x63 -> x0, matrix products: 129 us -> none  [the longest x39 79.4 us: matmul(): return jnp.dot(a, b, preferred_element_type=jnp.float32)]
    dynamic_update_slice x16 -> x0, local copies, waits for them, and re-layouts: 66.1 us -> none  [one_block(): return lax.dynamic_update_slice_in_dim(total, current + contrib, base, 0)]
    another operation x6 -> x0, loops' own time: 62.9 us -> none  [the longest x2 31.4 us: window_add(): lax.fori_loop(0, blocks.shape[0], one_block, jnp.zeros((rows + block, wid...]
    another operation x4 -> x0, other arithmetic: 57.9 us -> none  [the longest x1 28.8 us: shards(): jnp.full((compact,), band_rows_count, jnp.int32).at[rank]]
    all_to_all x5 -> x0, waiting for transfers between devices: 39.7 us -> none  [the longest x1 18.9 us: shards(): lax.all_to_all(partial_value.reshape(owners, CAP, width), 'mesh', split_a...]
    scatter-add x5 -> x0, other arithmetic: 37.4 us -> none  [the longest x2 17.2 us: shards(): jnp.zeros((compact, width), jnp.float32).at[slot_of]]
  transfers between devices with their start and end apart: 6 -> 0, of which waited for: 4 -> 0; matrix products, arithmetic and copies ran while one was open for 5% -> 0% of each run, Pallas kernels for 0% -> 0%
where the time goes in v1:
time: 154 us
  Pallas kernels  145 us (94%)
  local copies, waits for them, and re-layouts  7.78 us (5%)
    pallas_call x1, Pallas kernels, shards(): pl.pallas_call(functools.partial(reduce_kernel, nb, nm, scale), out_shape...  48 us
    pallas_call x1, Pallas kernels, shards(): pl.pallas_call(functools.partial(node_kernel, nm), out_shape=(shape((mesh...  34.8 us
    pallas_call x1, Pallas kernels, shards(): pl.pallas_call(functools.partial(fetch_kernel, nb, nm), out_shape=(shape(...  26.5 us
    pallas_call x1, Pallas kernels, shards(): pl.pallas_call(edge_kernel, out_shape=(shape((slots_n, width), BF16), sha...  21.6 us
    pallas_call x1, Pallas kernels, shards(): pl.pallas_call(grid_kernel, out_shape=shape((width, width), BF16), in_spe...  14.2 us
    unnamed x14, local copies, waits for them, and re-layouts  7.78 us

profile of v1, /device:TPU:1, one launch (start us, length us, event | category | flops | bytes accessed | tf_op | source)
XLA Modules:
  0.0 153.6 jit_solution(3379700588117301514)
XLA Ops:
  0.6 2.0 %copy.22.gv = bf16[1024,227]{1,0:T(8,128)(2,1)} copy(bf16[1024,227]{0,1:T(8,128)(2,1)} %param.17) | data formatting | bytes 929792 | tf_op args[0]
  2.7 26.5 %fetch.1 = (bf16[768,512]{1,0:T(8,128)(2,1)}, bf16[768,384]{1,0:T(8,128)(2,1)}, bf16[1024,512]{1,0:T(8,128)(2,1)}, bf16[1024,512]{1,0:T(8,128)(2,1)}, s32[32,128...) custom-call(s32[32,128]{1,0:T(8,128)} %bitcast.10, s32[32,128]{1,0:T(8,128)} %bitcast.11, ...), custom_call_target="tpu_custom_call" | custom-call | tf_op jit(solution)/shard_map/fetch/pallas_call | solution.py:396
  29.2 21.6 %edges.1 = (bf16[768,512]{1,0:T(8,128)(2,1)}, bf16[768,512]{1,0:T(8,128)(2,1)}, bf16[4096,512]{1,0:T(8,128)(2,1)}) custom-call(s32[32,128]{1,0:T(8,128)} %get-tuple-element.24.slot_s.slots, s32[32,128]{1,0:T(8,128)} %get-tuple-element.24.slot_s.slots, s32[32,128]{1,0:T(8,128)} %get-tuple-element.25.grid_rows, s32[4096,128]{1,0:T(8,128)} %get-tuple-element.26.slot_col, ...), custom_call_target="tpu_custom_call" | custom-call | tf_op jit(solution)/shard_map/edges/pallas_call | solution.py:417
  50.8 34.8 %nodes.1 = (bf16[320,512]{1,0:T(8,128)(2,1)}, bf16[320,512]{1,0:T(8,128)(2,1)}, bf16[768,512]{1,0:T(8,128)(2,1)}, bf16[512,512]{1,0:T(8,128)(2,1)}, bf16[512,512]{1,0:T(8,128)(2,1)}) custom-call(bf16[16,48,512]{2,1,0:T(8,128)(2,1)} %bitcast.8, bf16[16,48,512]{2,1,0:T(8,128)(2,1)} %bitcast.9, bf16[768,384]{1,0:T(8,128)(2,1)} %get-tuple-element.32.pick, ...), custom_call_target="tpu_custom_call" | custom-call | tf_op jit(solution)/shard_map/nodes/pallas_call | solution.py:429
  85.5 0.0 copy-start.3
  85.6 14.2 %grids.1.gg = bf16[512,512]{1,0:T(8,128)(2,1)} custom-call(s32[32,128]{1,0:T(8,128)} %get-tuple-element.24.slot_s.slots, s32[32,128]{1,0:T(8,128)} %get-tuple-element.25.grid_rows, s32[4096,128]{1,0:T(8,128)} %get-tuple-element.26.slot_col, bf16[768,512]{1,0:T(8,128)(2,1)} %get-tuple-element.37.htable, bf16[4096,512]{1,0:T(8,128)(2,1)} %get-tuple-element.38.slope, ...), custom_call_target="tpu_custom_call" | custom-call | tf_op jit(solution)/shard_map/grids/pallas_call | solution.py:442
  99.8 0.0 copy-start.2
  99.8 48.0 %reduce.1 = (f32[512,512]{1,0:T(8,128)}, f32[512,512]{1,0:T(8,128)}, f32[512,512]{1,0:T(8,128)}) custom-call(bf16[512,512]{1,0:T(8,128)(2,1)} %get-tuple-element.35.ge, bf16[512,512]{1,0:T(8,128)(2,1)} %get-tuple-element.36.gu, bf16[512,512]{1,0:T(8,128)(2,1)} %grids.1.gg), custom_call_target="tpu_custom_call" | custom-call | tf_op jit(solution)/shard_map/reduce/pallas_call | solution.py:465
  147.8 0.0 copy-start.1
  147.8 0.0 copy-done.3
  147.8 0.7 copy.28
  148.6 0.0 copy-done.2
  148.6 0.7 copy.29
  149.3 0.0 copy-start
  149.3 2.4 %copy.30 = f32[512,512]{1,0:T(8,128)} copy(f32[512,512]{1,0:T(8,128)} %get-tuple-element.50) | data formatting | bytes 2097152
  151.6 0.0 copy-done.1
  151.6 1.0 copy.31
  152.6 0.0 copy-done
  152.6 1.0 copy.32
Async XLA Ops:
  85.5 62.3 %copy-start.3 = (bf16[320,512]{1,0:T(8,128)(2,1)S(1)}, bf16[320,512]{1,0:T(8,128)(2,1)}, u32[]{:S(2)}) copy-start(bf16[320,512]{1,0:T(8,128)(2,1)} %get-tuple-element.48) | copy-start | bytes 983044
  99.8 48.8 %copy-start.2 = (bf16[320,512]{1,0:T(8,128)(2,1)S(1)}, bf16[320,512]{1,0:T(8,128)(2,1)}, u32[]{:S(2)}) copy-start(bf16[320,512]{1,0:T(8,128)(2,1)} %get-tuple-element.49) | copy-start | bytes 983044
  147.8 3.8 %copy-start.1 = (f32[512,512]{1,0:T(8,128)S(1)}, f32[512,512]{1,0:T(8,128)}, u32[]{:S(2)}) copy-start(f32[512,512]{1,0:T(8,128)} %get-tuple-element.51) | copy-start | bytes 3145732
  149.3 3.3 %copy-start = (f32[512,512]{1,0:T(8,128)S(1)}, f32[512,512]{1,0:T(8,128)}, u32[]{:S(2)}) copy-start(f32[512,512]{1,0:T(8,128)} %get-tuple-element.52) | copy-start | bytes 3145732

commit v2 on v1

--- a/solution.py
+++ b/solution.py
@@ -91,7 +91,7 @@
     local_grid, left, right, ids_out, ids_in, asked, landed, pmesh, s1, r1, s2, r2,
 ):
     mesh_dev = ml.shape[0]
-    grid_dev = gv.shape[0]
+    grid_dev = gv.shape[1]
     rows = em.shape[0]
     me = lax.axis_index("mesh")
     band = lax.axis_index("band")
@@ -155,7 +155,7 @@
 
     def grid_rows(i, carry):
         cut = pl.ds(pl.multiple_of(i * step, step), step)
-        v = dot(gv[cut, :], w_in[...]) + b_in[...]
+        v = dot_tn(gv[:, cut], w_in[...]) + b_in[...]
         hidden = (v * sigmoid(v)).astype(BF16)
         y = dot(hidden, w_out[...])
         centred = y - jnp.mean(y, axis=-1, keepdims=True)
@@ -222,26 +222,127 @@
 
     lax.fori_loop(0, rows // per, block, 0)
     a_out[...] = acc[:, 0:width].astype(BF16)
-    s_out[...] = acc[:, width:].astype(BF16)
-
-
-def node_kernel(
-    nm, a_part, s_part, pick, ml, ct, w_edge, w_self, w_agg, b_node, w_node, u_mesh,
-    mesh_out, grad_mesh, htable, g_edge, g_umesh,
-    a_in, s_in, asked, landed, s1, r1, s2, r2, s3, r3,
+    half = width // 2
+    for c in range(2):
+        s_out[c] = acc[:, width + c * half : width + (c + 1) * half].astype(BF16)
+
+
+def make_sum(axes, scale, big, small, width, in1, mid, in2, own, all2, all1, q1, q2, q3, q4):
+    n, m = axes[big], axes[small]
+    rows = in1.shape[1]
+    pr, pc = mid.shape[1], mid.shape[2]
+    cols = width // pc
+    live = {}
+
+    def start(src):
+        def part(p):
+            return src.at[pl.ds(pl.multiple_of(p * rows, 16), rows), :]
+
+        live[1] = send_all(big, n, part, lambda q: in1.at[q], q1.at[0], q1.at[1])
+        me = lax.axis_index(big)
+        in1[me] = src[pl.ds(pl.multiple_of(me * rows, 16), rows), :]
+
+    def middle():
+        wait_all(live[1])
+        total = in1[0].astype(F32)
+        for q in range(1, n):
+            total = total + in1[q].astype(F32)
+        for i in range(m):
+            a, c = i // cols, i % cols
+            mid[i] = total[a * pr : (a + 1) * pr, c * pc : (c + 1) * pc]
+        live[2] = send_all(small, m, lambda p: mid.at[p], lambda q: in2.at[q], q2.at[0], q2.at[1])
+        me = lax.axis_index(small)
+        in2[me] = mid[me]
+
+    def gather():
+        wait_all(live[2])
+        total = in2[0]
+        for q in range(1, m):
+            total = total + in2[q]
+        own[...] = total * scale
+        live[3] = send_all(small, m, lambda p: own, lambda q: all2.at[q], q3.at[0], q3.at[1])
+        all2[lax.axis_index(small)] = own[...]
+
+    def spread():
+        wait_all(live[3])
+        me = lax.axis_index(big)
+        bands = []
+        for a in range(m // cols):
+            bands.append(jnp.concatenate([all2[a * cols + c] for c in range(cols)], axis=1))
+        all1[me] = jnp.concatenate(bands, axis=0).astype(BF16)
+        live[4] = send_all(big, n, lambda p: all1.at[me], lambda q: all1.at[q], q4.at[0], q4.at[1])
+
+    def finish(out):
+        wait_all(live[4])
+        out[...] = all1[...].reshape(out.shape)
+
+    return start, middle, gather, spread, finish
+
+
+GB = 1024
+
+
+def back_kernel(
+    nb, nm, scale, pick, ml, ct, b_node, grid_rows, a_part, s_part, w_edge_h, w_self_h, w_agg_h,
+    w_node_h, u_mesh_h, slot_col_h, slope_h, latent_h,
+    mesh_out, grad_mesh, oe, ou, o0, o1,
+    w_edge, w_self, w_agg, w_node, u_mesh, slot_col, slope, latent, load_sem, self_sem,
+    a_in, s_in, asked, landed, hot_s, hot_g, acc, ge, gu, g0, g1,
+    sa, ra, ss, rs, sh, rh, *sums,
 ):
-    mesh_dev = ml.shape[0]
+    mesh_dev, width = ml.shape
+    half = width // 2
+    rows = grid_rows.shape[0]
     me = lax.axis_index("mesh")
-    enter((("mesh", nm),))
-    sent_a = send_all("mesh", nm, lambda p: a_part.at[p], lambda q: a_in.at[q], s1, r1)
-    sent_s = send_all("mesh", nm, lambda p: s_part.at[p], lambda q: s_in.at[q], s2, r2)
-    a_in[me] = a_part[me]
-    s_in[me] = s_part[me]
-    flat = (a_in.shape[0] * a_in.shape[1], a_in.shape[2])
+    axes = {"band": nb, "mesh": nm}
+    plans = [
+        make_sum(axes, scale, big, small, w, *sums[i * 10 : (i + 1) * 10])
+        for i, (big, small, w) in enumerate(
+            (("band", "mesh", width), ("band", "mesh", width), ("mesh", "band", half), ("mesh", "band", half))
+        )
+    ]
+    enter((("mesh", nm), ("band", nb)))
+    sent_a = send_all("mesh", nm, lambda p: a_part.at[p], lambda q: a_in.at[q], sa, ra)
+    own_a = pltpu.make_async_copy(a_part.at[me], a_in.at[me], self_sem.at[0])
+    own_a.start()
+    loads = []
+    for i, (src, dst) in enumerate(
+        ((w_self_h, w_self), (w_node_h, w_node), (slot_col_h, slot_col), (w_edge_h, w_edge), (w_agg_h, w_agg),
+         (u_mesh_h, u_mesh), (slope_h, slope), (latent_h, latent))
+    ):
+        copy = pltpu.make_async_copy(src, dst, load_sem.at[i])
+        copy.start()
+        loads.append(copy)
+    sent_s, own_s = [], []
+    for c in range(2):
+        if c == 0:
+            sent_s.append(send_all("mesh", nm, lambda p: s_part.at[0, p], lambda q: s_in.at[0, q], ss.at[0], rs.at[0]))
+        copy = pltpu.make_async_copy(s_part.at[c, me], s_in.at[c, me], self_sem.at[1 + c])
+        copy.start()
+        own_s.append(copy)
+    loads[0].wait()
     own = dot(ml[...], w_self[...]) + b_node[...]
+    loads[1].wait()
     back = dot_nt(ct[...], w_node[...])
+    loads[2].wait()
+    slots_n = hot_s.shape[1]
+    grid_dev = hot_g.shape[0]
+
+    def build(r, carry):
+        cut = pl.ds(pl.multiple_of(r * 128, 128), 128)
+        scol = slot_col[cut, :]
+        for t in range(slots_n // 128):
+            hot_s[cut, t * 128 : (t + 1) * 128] = onehot(scol == iota((128, 128), 1) + t * 128)
+        hot_g[:, cut] = onehot(grid_rows[pl.ds(r, 1), :] == iota((grid_dev, 128), 0))
+        return carry
+
+    lax.fori_loop(0, rows, build, 0)
+    for copy in loads[3:5]:
+        copy.wait()
+    own_a.wait()
     wait_all(sent_a)
-    acts = dot_tn(pick[...], a_in[...].reshape(flat))[0:mesh_dev].astype(BF16)
+    flat = nm * CAP
+    acts = dot_tn(pick[...], a_in[...].reshape(flat, width))[0:mesh_dev].astype(BF16)
     agg = dot(acts, w_edge[...]).astype(BF16)
     node_pre = own + dot(agg, w_agg[...])
     s = sigmoid(node_pre)
@@ -250,118 +351,79 @@
     g_agg = dot_nt(g_node, w_agg[...]).astype(BF16)
     h = dot_nt(g_agg, w_edge[...])
     hb = jnp.concatenate(
-        [h.astype(BF16), jnp.zeros((pick.shape[1] - mesh_dev, h.shape[1]), BF16)], axis=0
+        [h.astype(BF16), jnp.zeros((pick.shape[1] - mesh_dev, width), BF16)], axis=0
     )
-    asked[...] = dot(pick[...], hb).astype(BF16).reshape(asked.shape)
-    sent_h = send_all("mesh", nm, lambda p: asked.at[p], lambda q: landed.at[q], s3, r3)
-    landed[me] = asked[me]
+    sent_h = []
+    for c in range(2):
+        asked[c] = dot(pick[...], hb[:, c * half : (c + 1) * half]).astype(BF16).reshape(nm, CAP, half)
+        sent_h.append(send_all("mesh", nm, lambda p, c=c: asked.at[c, p], lambda q, c=c: landed.at[c, q],
+                               sh.at[c], rh.at[c]))
+        landed[c, me] = asked[c, me]
+    sent_s.append(send_all("mesh", nm, lambda p: s_part.at[1, p], lambda q: s_in.at[1, q], ss.at[1], rs.at[1]))
+    ge[...] = dot_tn(acts, g_agg).astype(BF16)
+    plans[0][0](ge)
     mesh_out[...] = (ml[...].astype(F32) + dot(node_act.astype(BF16), w_node[...])).astype(BF16)
-    g_edge[...] = dot_tn(acts, g_agg).astype(BF16)
     part = ct[...].astype(F32) + dot_nt(g_node, w_self[...])
-    wait_all(sent_s)
-    slopes = dot_tn(pick[...], s_in[...].reshape(flat))[0:mesh_dev]
+    for copy in loads[5:]:
+        copy.wait()
+
+    def grid_half(c):
+        acc[...] = jnp.zeros_like(acc)
+        col = slice(c * half, (c + 1) * half)
+        table = landed[c].reshape(flat, half)
+
+        def block(b, carry):
+            cut = pl.ds(pl.multiple_of(b * GB, GB), GB)
+            g = (dot(hot_s[cut, :], table) * slope[cut, col].astype(F32)).astype(BF16)
+            acc[...] += dot(hot_g[:, cut], g)
+            return carry
+
+        lax.fori_loop(0, rows * 128 // GB, block, 0)
+        return dot_tn(latent[...], acc[...].astype(BF16)).astype(BF16)
+
+    wait_all(sent_h[0])
+    g0[...] = grid_half(0)
+    plans[2][0](g0)
+    wait_all(sent_h[1])
+    plans[0][1]()
+    g1[...] = grid_half(1)
+    plans[3][0](g1)
+    for copy in own_s:
+        copy.wait()
+    wait_all(sent_s[0])
+    wait_all(sent_s[1])
+    slopes = jnp.concatenate(
+        [dot_tn(pick[...], s_in[c].reshape(flat, half))[0:mesh_dev] for c in range(2)], axis=1
+    )
     g_pmesh = (h * slopes).astype(BF16)
-    g_umesh[...] = dot_tn(ml[...], g_pmesh).astype(BF16)
+    gu[...] = dot_tn(ml[...], g_pmesh).astype(BF16)
+    plans[1][0](gu)
     grad_mesh[...] = (part + dot_nt(g_pmesh, u_mesh[...])).astype(BF16)
-    wait_all(sent_h)
-    htable[...] = landed[...].reshape(htable.shape)
-
-
-def grid_kernel(slot_s, grid_rows, slot_col, htable, slope, latent, g_ugrid, acc, pre):
-    rows = grid_rows.shape[0]
-    tiles = htable.shape[0] // TB
-    per = EB // 128
-    acc[...] = jnp.zeros_like(acc)
-
-    def block(b, carry):
-        cut = pl.ds(pl.multiple_of(b * EB, EB), EB)
-        low = slot_s[b * per, 0]
-        high = slot_s[b * per + per - 1, 127]
-        pre[...] = jnp.zeros_like(pre)
-        for t in range(tiles):
-            @pl.when((low < (t + 1) * TB) & (high >= t * TB))
-            def _():
-                scol = slot_col[cut, :]
-                hot = jnp.concatenate(
-                    [onehot(scol == iota((EB, 128), 1) + (t * TB + u * 128)) for u in range(TB // 128)],
-                    axis=1,
-                )
-                pre[...] += dot(hot, htable[t * TB : (t + 1) * TB, :])
-
-        g = (pre[...] * slope[cut, :].astype(F32)).astype(BF16)
-        n = acc.shape[0]
-        hot = jnp.concatenate(
-            [onehot(grid_rows[pl.ds(b * per + u, 1), :] == iota((n, 128), 0)) for u in range(per)],
-            axis=1,
-        )
-        acc[...] += dot(hot, g)
-        return carry
-
-    lax.fori_loop(0, rows // per, block, 0)
-    g_ugrid[...] = dot_tn(latent[...], acc[...].astype(BF16)).astype(BF16)
-
-
-def reduce_kernel(nb, nm, scale, ge, gu, gg, oe, ou, og, *scratch):
-    axes = {"band": nb, "mesh": nm}
-    enter((("band", nb), ("mesh", nm)))
-    width = ge.shape[1]
-    plans = []
-    for i, (src, out) in enumerate(((ge, oe), (gu, ou), (gg, og))):
-        big, small = ("mesh", "band") if i == 2 else ("band", "mesh")
-        plans.append((src, out, big, small) + tuple(scratch[i * 10 : (i + 1) * 10]))
-    stage = []
-    for src, out, big, small, in1, mid, in2, own, all2, all1, *sems in plans:
-        n = axes[big]
-        rows = in1.shape[1]
-        stage.append(send_all(
-            big, n,
-            lambda p, src=src, rows=rows: src.at[pl.ds(pl.multiple_of(p * rows, 16), rows), :],
-            lambda q, in1=in1: in1.at[q], sems[0].at[0], sems[0].at[1]))
-        me = lax.axis_index(big)
-        in1[me] = src[pl.ds(pl.multiple_of(me * rows, 16), rows), :]
-    nxt = []
-    for k, (src, out, big, small, in1, mid, in2, own, all2, all1, *sems) in enumerate(plans):
-        wait_all(stage[k])
-        n, m = axes[big], axes[small]
-        total = in1[0].astype(F32)
-        for q in range(1, n):
-            total = total + in1[q].astype(F32)
-        total = total.astype(BF16)
-        pr, pc = mid.shape[1], mid.shape[2]
-        cols = width // pc
-        for i in range(m):
-            a, c = i // cols, i % cols
-            mid[i] = total[a * pr : (a + 1) * pr, c * pc : (c + 1) * pc]
-        nxt.append(send_all(small, m, lambda p, mid=mid: mid.at[p], lambda q, in2=in2: in2.at[q],
-                            sems[1].at[0], sems[1].at[1]))
-        me = lax.axis_index(small)
-        in2[me] = mid[me]
-    stage, nxt = nxt, []
-    for k, (src, out, big, small, in1, mid, in2, own, all2, all1, *sems) in enumerate(plans):
-        wait_all(stage[k])
-        m = axes[small]
-        total = in2[0].astype(F32)
-        for q in range(1, m):
-            total = total + in2[q].astype(F32)
-        own[...] = (total * scale).astype(BF16)
-        nxt.append(send_all(small, m, lambda p, own=own: own, lambda q, all2=all2: all2.at[q],
-                            sems[2].at[0], sems[2].at[1]))
-        all2[lax.axis_index(small)] = own[...]
-    stage, nxt = nxt, []
-    for k, (src, out, big, small, in1, mid, in2, own, all2, all1, *sems) in enumerate(plans):
-        wait_all(stage[k])
-        n, m = axes[big], axes[small]
-        pr, pc = mid.shape[1], mid.shape[2]
-        cols = width // pc
-        me = lax.axis_index(big)
-        for i in range(m):
-            a, c = i // cols, i % cols
-            all1[me, a * pr : (a + 1) * pr, c * pc : (c + 1) * pc] = all2[i]
-        nxt.append(send_all(big, n, lambda p, all1=all1, me=me: all1.at[me], lambda q, all1=all1: all1.at[q],
-                            sems[3].at[0], sems[3].at[1]))
-    for k, (src, out, big, small, in1, mid, in2, own, all2, all1, *sems) in enumerate(plans):
-        wait_all(nxt[k])
-        out[...] = all1[...].reshape(out.shape).astype(F32)
+    plans[2][1]()
+    plans[0][2]()
+    plans[3][1]()
+    plans[1][1]()
+    plans[2][2]()
+    plans[0][3]()
+    plans[3][2]()
+    plans[1][2]()
+    plans[2][3]()
+    plans[3][3]()
+    plans[1][3]()
+    plans[0][4](oe)
+    plans[2][4](o0)
+    plans[3][4](o1)
+    plans[1][4](ou)
+
+
+def write_kernel(mo, gm, e, u, g0, g1, mo_out, gm_out, e_out, g_out, u_out):
+    half = g0.shape[1]
+    mo_out[...] = mo[...]
+    gm_out[...] = gm[...]
+    e_out[...] = e[...].astype(F32)
+    u_out[...] = u[...].astype(F32)
+    g_out[:, 0:half] = g0[...].astype(F32)
+    g_out[:, half:] = g1[...].astype(F32)
 
 
 def vmem():
@@ -412,11 +474,13 @@
         ],
         compiler_params=params(0),
         name="fetch",
-    )(em, eg, grid_vars, mesh_latent, w_in, b_in.reshape(1, -1), w_out, norm_gain.reshape(1, -1),
+    )(em, eg, grid_vars.T, mesh_latent, w_in, b_in.reshape(1, -1), w_out, norm_gain.reshape(1, -1),
       u_grid, u_mesh)
     a_part, s_part, slope = pl.pallas_call(
         edge_kernel,
-        out_shape=(shape((slots_n, width), BF16), shape((slots_n, width), BF16), shape((edges, width), BF16)),
+        out_shape=(
+            shape((slots_n, width), BF16), shape((2, slots_n, width // 2), BF16), shape((edges, width), BF16),
+        ),
         in_specs=[pl.BlockSpec(memory_space=pltpu.SMEM)] + [vmem()] * 7,
         out_specs=(vmem(),) * 3,
         scratch_shapes=[
@@ -426,52 +490,51 @@
         compiler_params=params(),
         name="edges",
     )(slots, slots, local_grid, slot_col, grid_col, table, pgrid, b_edge.reshape(1, -1))
-    mesh_out, grad_mesh, htable, g_edge, g_umesh = pl.pallas_call(
-        functools.partial(node_kernel, nm),
-        out_shape=(
-            shape((mesh_dev, width), BF16), shape((mesh_dev, width), BF16), shape((slots_n, width), BF16),
-            shape((width, width), BF16), shape((width, width), BF16),
-        ),
-        in_specs=[vmem()] * 11,
-        out_specs=(vmem(),) * 5,
-        scratch_shapes=[pltpu.VMEM((nm, CAP, width), BF16)] * 4 + [sem((nm,))] * 6,
-        compiler_params=params(1),
-        name="nodes",
-    )(a_part.reshape(nm, CAP, width), s_part.reshape(nm, CAP, width), pick, mesh_latent, cotangent,
-      w_edge, w_self, w_agg, b_node.reshape(1, -1), w_node_out, u_mesh)
-    g_ugrid = pl.pallas_call(
-        grid_kernel,
-        out_shape=shape((width, width), BF16),
-        in_specs=[pl.BlockSpec(memory_space=pltpu.SMEM)] + [vmem()] * 5,
-        out_specs=vmem(),
-        scratch_shapes=[pltpu.VMEM((grid_dev, width), F32), pltpu.VMEM((EB, width), F32)],
-        compiler_params=params(),
-        name="grids",
-    )(slots, local_grid, slot_col, htable, slope, latent)
-    scratch = []
-    for i in range(3):
-        n, m = (nm, nb) if i == 2 else (nb, nm)
+    half = width // 2
+    sums = []
+    for n, m, w in ((nb, nm, width), (nb, nm, width), (nm, nb, half), (nm, nb, half)):
         big = width // n
-        pc = min(4, m)
-        piece = (big // (m // pc), width // pc)
-        scratch += [
-            pltpu.VMEM((n, big, width), BF16), pltpu.VMEM((m,) + piece, BF16),
-            pltpu.VMEM((m,) + piece, BF16), pltpu.VMEM(piece, BF16), pltpu.VMEM((m,) + piece, BF16),
-            pltpu.VMEM((n, big, width), BF16),
+        across = min(m, w // 128)
+        piece = (big // (m // across), w // across)
+        sums += [
+            pltpu.VMEM((n, big, w), BF16), pltpu.VMEM((m,) + piece, F32),
+            pltpu.VMEM((m,) + piece, F32), pltpu.VMEM(piece, F32), pltpu.VMEM((m,) + piece, F32),
+            pltpu.VMEM((n, big, w), BF16),
             sem((2, n)), sem((2, m)), sem((2, m)), sem((2, n)),
         ]
     scale = (edges * nb * nm) ** (-0.5)
-    out = shape((width, width), F32)
-    grad_edge, grad_umesh, grad_ugrid = pl.pallas_call(
-        functools.partial(reduce_kernel, nb, nm, scale),
-        out_shape=(out, out, out),
-        in_specs=[vmem()] * 3,
-        out_specs=(vmem(),) * 3,
-        scratch_shapes=scratch,
-        compiler_params=params(2),
-        name="reduce",
-    )(g_edge, g_umesh, g_ugrid)
-    return (mesh_out, grad_mesh, grad_edge, grad_ugrid, grad_umesh)
+    node = shape((mesh_dev, width), BF16)
+    square = shape((width, width), BF16)
+    slim = shape((width, half), BF16)
+    matrix = pltpu.VMEM((width, width), BF16)
+    outs = pl.pallas_call(
+        functools.partial(back_kernel, nb, nm, scale),
+        out_shape=(node, node, square, square, slim, slim),
+        in_specs=[vmem()] * 5 + [pl.BlockSpec(memory_space=pl.ANY)] * 10,
+        out_specs=(vmem(),) * 6,
+        scratch_shapes=[matrix] * 5 + [
+            pltpu.VMEM((edges, 128), jnp.int32), pltpu.VMEM((edges, width), BF16),
+            pltpu.VMEM((grid_dev, width), BF16), sem((8,)), sem((3,)),
+            pltpu.VMEM((nm, CAP, width), BF16), pltpu.VMEM((2, nm, CAP, half), BF16),
+            pltpu.VMEM((2, nm, CAP, half), BF16), pltpu.VMEM((2, nm, CAP, half), BF16),
+            pltpu.VMEM((edges, slots_n), BF16), pltpu.VMEM((grid_dev, edges), BF16),
+            pltpu.VMEM((grid_dev, half), F32), matrix, matrix,
+            pltpu.VMEM((width, half), BF16), pltpu.VMEM((width, half), BF16),
+            sem((nm,)), sem((nm,)), sem((2, nm)), sem((2, nm)), sem((2, nm)), sem((2, nm)),
+        ] + sums,
+        compiler_params=params(1),
+        name="back",
+    )(pick, mesh_latent, cotangent, b_node.reshape(1, -1), local_grid, a_part.reshape(nm, CAP, width),
+      s_part.reshape(2, nm, CAP, half), w_edge, w_self, w_agg, w_node_out, u_mesh, slot_col, slope, latent)
+    final = shape((width, width), F32)
+    return pl.pallas_call(
+        write_kernel,
+        out_shape=(node, node, final, final, final),
+        in_specs=[vmem()] * 6,
+        out_specs=(vmem(),) * 5,
+        compiler_params=params(),
+        name="write",
+    )(*outs)
 
 
 def solution(mesh):

time: 154 us -> 135 us (0.88)
  Pallas kernels: 145 us -> 134 us
  local copies, waits for them, and re-layouts: 7.78 us -> 0 us
    pallas_call x3 -> x2, Pallas kernels: 97 us -> 85.9 us  [the longest x1 82.4 us: shards(): pl.pallas_call(functools.partial(back_kernel, nb, nm, scale), out_shape=(...]
    unnamed x14 -> x0, local copies, waits for them, and re-layouts: 7.78 us -> none
where the time goes in v2:
time: 135 us
  Pallas kernels  134 us (99%)
    pallas_call x1, Pallas kernels, shards(): pl.pallas_call(functools.partial(back_kernel, nb, nm, scale), out_shape=(...  82.4 us
    pallas_call x1, Pallas kernels, shards(): pl.pallas_call(functools.partial(fetch_kernel, nb, nm), out_shape=(shape(...  26.6 us
    pallas_call x1, Pallas kernels, shards(): pl.pallas_call(edge_kernel, out_shape=(shape((slots_n, width), BF16), sha...  21.6 us
    pallas_call x1, Pallas kernels, shards(): pl.pallas_call(write_kernel, out_shape=(node, node, final, final, final),...  3.44 us

profile of v2, /device:TPU:1, one launch (start us, length us, event | category | flops | bytes accessed | tf_op | source)
XLA Modules:
  0.0 134.7 jit_solution(6425212996720227724)
XLA Ops:
  0.6 26.6 %fetch.1 = (bf16[768,512]{1,0:T(8,128)(2,1)}, bf16[768,384]{1,0:T(8,128)(2,1)}, bf16[1024,512]{1,0:T(8,128)(2,1)}, bf16[1024,512]{1,0:T(8,128)(2,1)}, s32[32,128...) custom-call(s32[32,128]{1,0:T(8,128)} %bitcast.12, s32[32,128]{1,0:T(8,128)} %bitcast.13, ...), custom_call_target="tpu_custom_call" | custom-call | tf_op jit(solution)/shard_map/fetch/pallas_call | solution.py:458
  27.2 21.6 %edges.1 = (bf16[768,512]{1,0:T(8,128)(2,1)}, bf16[2,768,256]{2,1,0:T(8,128)(2,1)}, bf16[4096,512]{1,0:T(8,128)(2,1)}) custom-call(s32[32,128]{1,0:T(8,128)} %get-tuple-element.24.slot_s.slots, s32[32,128]{1,0:T(8,128)} %get-tuple-element.24.slot_s.slots, s32[32,128]{1,0:T(8,128)} %get-tuple-element.23.grid_rows, ...), custom_call_target="tpu_custom_call" | custom-call | tf_op jit(solution)/shard_map/edges/pallas_call | solution.py:479
  48.8 82.4 %back.1 = (bf16[320,512]{1,0:T(8,128)(2,1)}, bf16[320,512]{1,0:T(8,128)(2,1)}, bf16[512,512]{1,0:T(8,128)(2,1)}, bf16[512,512]{1,0:T(8,128)(2,1)}, bf16[512,256]{1,0:T(8,128)(2,1)}, /*index=5*/bf16[512,256]{1,0:T(8,128)(2,1)}) custom-call(bf16[768,384]{1,0:T(8,128)(2,1)} %get-tuple-element.22.pick, bf16[320,512]{1,0:T(8,128)(2,1)} %ml.3, ...), custom_call_target="tpu_custom_call" | custom-call | tf_op jit(solution)/shard_map/back/pallas_call | solution.py:510
  131.2 3.4 %write.1 = (bf16[320,512]{1,0:T(8,128)(2,1)}, bf16[320,512]{1,0:T(8,128)(2,1)}, f32[512,512]{1,0:T(8,128)}, f32[512,512]{1,0:T(8,128)}, f32[512,512]{1,0:T(8,128)}) custom-call(bf16[320,512]{1,0:T(8,128)(2,1)} %get-tuple-element.33.mo, bf16[320,512]{1,0:T(8,128)(2,1)} %get-tuple-element.34.gm, bf16[512,512]{1,0:T(8,128)(2,1)} %get-tuple-element.35.e, ...), custom_call_target="tpu_custom_call" | custom-call | tf_op jit(solution)/shard_map/write/pallas_call | solution.py:530

commit v3 on v2

v3 whole, which is shorter than its diff:
```python
import functools

import jax
import jax.numpy as jnp
from jax import lax
from jax.experimental import pallas as pl
from jax.experimental.pallas import tpu as pltpu
from jax.sharding import PartitionSpec as P

CAP = 48
MESH = pl.DeviceIdType.MESH
F32 = jnp.float32
BF16 = jnp.bfloat16
MIB = 1024 * 1024


EB = 512
TB = 256


def sigmoid(v):
    return 0.5 + 0.5 * jnp.tanh(0.5 * v)


def dot(a, b):
    return jnp.dot(a, b, preferred_element_type=F32)


def dot_nt(a, b):
    return lax.dot_general(a, b, (((1,), (1,)), ((), ())), preferred_element_type=F32)


def dot_tn(a, b):
    return lax.dot_general(a, b, (((0,), (0,)), ((), ())), preferred_element_type=F32)


def iota(shape, dim):
    return lax.broadcasted_iota(jnp.int32, shape, dim)


def onehot(mask):
    return jnp.where(mask, 1.0, 0.0).astype(BF16)


def enter(axes):
    barrier = pltpu.get_barrier_semaphore()
    total = 0
    for axis, n in axes:
        me = lax.axis_index(axis)
        for d in range(1, n):
            pl.semaphore_signal(
                barrier, inc=1, device_id={axis: lax.rem(me + d, n)}, device_id_type=MESH
            )
        total += n - 1
    pl.semaphore_wait(barrier, total)


def send_all(axis, n, src, dst, send_sem, recv_sem):
    me = lax.axis_index(axis)
    copies = []
    for d in range(1, n):
        peer = lax.rem(me + d, n)
        copy = pltpu.make_async_remote_copy(
            src_ref=src(peer),
            dst_ref=dst(me),
            send_sem=send_sem.at[d],
            recv_sem=recv_sem.at[d],
            device_id={axis: peer},
            device_id_type=MESH,
        )
        copy.start()
        copies.append(copy)
    return copies


def wait_all(copies):
    for copy in copies:
        copy.wait()


def columns(rows_ref, out_ref):
    rows = rows_ref.shape[0]
    values = rows_ref[...].astype(F32)
    pad = jnp.zeros((128 - rows, 128), F32)
    turned = jnp.transpose(jnp.concatenate([values, pad], axis=0))
    for r in range(rows):
        out_ref[r * 128 : (r + 1) * 128, :] = jnp.broadcast_to(
            turned[:, r : r + 1], (128, 128)
        ).astype(jnp.int32)


def fetch_kernel(
    nb, nm, em, eg, gv, ml, w_in, b_in, w_out, gain, u_grid, u_mesh,
    table, rows_in, pick, latent_t, pre_grid, slots, slot_col, local_grid,
    grid_col, pgrid, left, right, ids_out, ids_in, asked, landed, padded, s1, r1, s2, r2,
):
    mesh_dev = ml.shape[0]
    grid_dev = gv.shape[1]
    rows = em.shape[0]
    me = lax.axis_index("mesh")
    band = lax.axis_index("band")
    enter((("mesh", nm),))
    x = em[...] - band * (nm * mesh_dev)
    lane = iota(x.shape, 1)
    row = iota(x.shape, 0)
    prev = pltpu.roll(x, 1, 1)
    prev = jnp.where(lane == 0, pltpu.roll(prev, 1, 0), prev)
    fresh = jnp.where((x != prev) | ((lane == 0) & (row == 0)), 1.0, 0.0)
    fb = fresh.astype(BF16)
    upper = onehot(iota((128, 128), 0) <= iota((128, 128), 1))
    totals = dot(fb, jnp.ones((128, 128), BF16)).astype(BF16)
    lower = onehot(iota((rows, rows), 1) < iota((rows, rows), 0))
    rank = dot(fb, upper) + dot(lower, totals) - 1.0
    owner = jnp.zeros(x.shape, jnp.int32)
    first = jnp.zeros(x.shape, F32)
    for o in range(1, nm):
        later = x >= o * mesh_dev
        begun = jnp.sum(jnp.where(later, 0.0, fresh), keepdims=True)
        owner = owner + jnp.where(later, 1, 0)
        first = jnp.where(later, begun, first)
    inner = (rank - first).astype(jnp.int32)
    slots[...] = owner * CAP + inner
    node = x - owner * mesh_dev
    high = jnp.right_shift(node, 4)
    low = node - high * 16
    high = jnp.where(fresh > 0, high, 0).astype(F32)
    low = jnp.where(fresh > 0, low, 0).astype(F32)
    owner_id = iota((nm, 128), 0)
    inner_id = iota((128, 128), 0)
    for r in range(rows):
        cut = slice(r * 128, (r + 1) * 128)
        mine = owner[r : r + 1, :] == owner_id
        left[0:nm, cut] = jnp.where(mine, high[r : r + 1, :], 0.0).astype(BF16)
        left[nm : 2 * nm, cut] = jnp.where(mine, low[r : r + 1, :], 0.0).astype(BF16)
        right[:, cut] = onehot(inner[r : r + 1, :] == inner_id)
    both = dot_nt(left[...], right[...])
    ids = both[0:nm] * 16.0 + both[nm : 2 * nm]
    for o in range(nm):
        ids_out[o] = jnp.broadcast_to(ids[o : o + 1, :], (8, 128))
    sent = send_all("mesh", nm, lambda p: ids_out.at[p], lambda q: ids_in.at[q], s1, r1)
    ids_in[me] = ids_out[me]
    padded[0:mesh_dev, :] = ml[...]
    padded[mesh_dev:, :] = jnp.zeros((padded.shape[0] - mesh_dev, padded.shape[1]), BF16)
    columns(slots, slot_col)
    local_grid[...] = eg[...] - (band * nm + me) * grid_dev
    columns(local_grid, grid_col)
    wait_all(sent)
    turned = jnp.transpose(ids_in[...].reshape(nm * 8, 128))
    for q in range(nm):
        ids_q = jnp.broadcast_to(turned[0:CAP, q * 8 : q * 8 + 1], (CAP, 128)).astype(jnp.int32)
        for t in range(pick.shape[1] // 128):
            pick[q * CAP : (q + 1) * CAP, t * 128 : (t + 1) * 128] = onehot(
                ids_q == iota((CAP, 128), 1) + t * 128
            )
    asked[...] = dot(pick[...], padded[...]).astype(BF16).reshape(asked.shape)
    sent = send_all("mesh", nm, lambda p: asked.at[p], lambda q: landed.at[q], s2, r2)
    landed[me] = asked[me]
    step = 256

    def grid_rows(i, carry):
        cut = pl.ds(pl.multiple_of(i * step, step), step)
        v = dot_tn(gv[:, cut], w_in[...]) + b_in[...]
        hidden = (v * sigmoid(v)).astype(BF16)
        y = dot(hidden, w_out[...])
        centred = y - jnp.mean(y, axis=-1, keepdims=True)
        var = jnp.mean(centred * centred, axis=-1, keepdims=True)
        lat = centred * lax.rsqrt(var + 1e-05) * gain[...]
        latent_t[:, cut] = jnp.transpose(lat).astype(BF16)
        pgrid[cut, :] = dot(lat.astype(BF16), u_grid[...]).astype(BF16)
        return carry

    lax.fori_loop(0, grid_dev // step, grid_rows, 0)

    def grid_edges(b, carry):
        cut = pl.ds(pl.multiple_of(b * EB, EB), EB)
        gcol = grid_col[cut, :]
        hot = jnp.concatenate(
            [onehot(gcol == iota((EB, 128), 1) + t * 128) for t in range(grid_dev // 128)], axis=1
        )
        pre_grid[cut, :] = dot(hot, pgrid[...]).astype(BF16)
        return carry

    lax.fori_loop(0, rows * 128 // EB, grid_edges, 0)
    wait_all(sent)
    rows_in[...] = landed[...].reshape(rows_in.shape)
    table[...] = dot(rows_in[...], u_mesh[...]).astype(BF16)


def edge_kernel(slot_s, slots, slot_col, table, pre_grid, b_edge, a_out, s_out, slope, acc, pre, both):
    rows = slots.shape[0]
    width = table.shape[1]
    tiles = table.shape[0] // TB
    per = EB // 128
    acc[...] = jnp.zeros_like(acc)

    def block(b, carry):
        cut = pl.ds(pl.multiple_of(b * EB, EB), EB)
        pre[...] = pre_grid[cut, :].astype(F32) + b_edge[...]
        low = slot_s[b * per, 0]
        high = slot_s[b * per + per - 1, 127]
        for t in range(tiles):
            @pl.when((low < (t + 1) * TB) & (high >= t * TB))
            def _():
                scol = slot_col[cut, :]
                hot = jnp.concatenate(
                    [onehot(scol == iota((EB, 128), 1) + (t * TB + u * 128)) for u in range(TB // 128)],
                    axis=1,
                )
                pre[...] += dot(hot, table[t * TB : (t + 1) * TB, :])

        v = pre[...]
        s = sigmoid(v)
        act = v * s
        both[:, 0:width] = act.astype(BF16)
        sl = (s + act * (1.0 - s)).astype(BF16)
        both[:, width:] = sl
        slope[cut, :] = sl
        for t in range(tiles):
            @pl.when((low < (t + 1) * TB) & (high >= t * TB))
            def _():
                hot = jnp.concatenate(
                    [onehot(slots[pl.ds(b * per + u, 1), :] == iota((TB, 128), 0) + t * TB) for u in range(per)],
                    axis=1,
                )
                acc[t * TB : (t + 1) * TB, :] += dot(hot, both[...])

        return carry

    lax.fori_loop(0, rows // per, block, 0)
    a_out[...] = acc[:, 0:width].astype(BF16)
    half = width // 2
    for c in range(2):
        s_out[c] = acc[:, width + c * half : width + (c + 1) * half].astype(BF16)


def make_sum(axes, scale, big, small, width, in1, mid, in2, all2, all1, q1, q2, q3, q4):
    n, m = axes[big], axes[small]
    rows = in1.shape[1]
    live = {}

    def add(ref, count):
        total = ref[0].astype(F32)
        for q in range(1, count):
            total = total + ref[q].astype(F32)
        return total

    def start(src):
        def part(p):
            return src.at[pl.ds(pl.multiple_of(p * rows, 16), rows), :]

        live[1] = send_all(big, n, part, lambda q: in1.at[q], q1.at[0], q1.at[1])
        me = lax.axis_index(big)
        in1[me] = src[pl.ds(pl.multiple_of(me * rows, 16), rows), :]

    def spread_big(values):
        me = lax.axis_index(big)
        all1[me] = values.astype(BF16)
        live[4] = send_all(big, n, lambda p: all1.at[me], lambda q: all1.at[q], q4.at[0], q4.at[1])

    def finish(out):
        wait_all(live[4])
        out[...] = all1[...].reshape(out.shape)

    if small == "band":

        def middle():
            wait_all(live[1])
            mid[...] = add(in1, n).astype(BF16)
            live[2] = send_all(small, m, lambda p: mid, lambda q: in2.at[q], q2.at[0], q2.at[1])
            in2[lax.axis_index(small)] = mid[...]

        def gather():
            wait_all(live[2])
            spread_big(add(in2, m) * scale)

        return start, middle, gather, None, finish

    pr, pc = mid.shape[1], mid.shape[2]
    cols = width // pc

    def middle():
        wait_all(live[1])
        total = add(in1, n)
        for i in range(m):
            a, c = i // cols, i % cols
            mid[i] = total[a * pr : (a + 1) * pr, c * pc : (c + 1) * pc]
        live[2] = send_all(small, m, lambda p: mid.at[p], lambda q: in2.at[q], q2.at[0], q2.at[1])
        me = lax.axis_index(small)
        in2[me] = mid[me]

    def gather():
        wait_all(live[2])
        me = lax.axis_index(small)
        all2[me] = add(in2, m) * scale
        live[3] = send_all(small, m, lambda p: all2.at[me], lambda q: all2.at[q], q3.at[0], q3.at[1])

    def spread():
        wait_all(live[3])
        spread_big(jnp.concatenate(
            [jnp.concatenate([all2[a * cols + c] for c in range(cols)], axis=1) for a in range(m // cols)],
            axis=0,
        ))

    return start, middle, gather, spread, finish


GB = 1024


def back_kernel(
    nb, nm, scale, pick, ml, ct, b_node, grid_rows, a_part, s_part, w_edge, w_self, w_agg,
    w_node, u_mesh, slot_col, slope, latent_t, rows_in,
    mesh_out, grad_mesh, oe, ou0, ou1, og0, og1,
    a_in, s_in, asked, landed, hot_s, lat_e, rows_t, acc, ge, gg, gu,
    sa, ra, ss, rs, sh, rh, *sums,
):
    mesh_dev, width = ml.shape
    half = width // 2
    rows = grid_rows.shape[0]
    slots_n = hot_s.shape[1]
    grid_dev = latent_t.shape[1]
    flat = nm * CAP
    me = lax.axis_index("mesh")
    axes = {"band": nb, "mesh": nm}
    sum_e, sum_u0, sum_u1, sum_g0, sum_g1 = [
        make_sum(axes, scale, big, small, w, *sums[i * 9 : (i + 1) * 9])
        for i, (big, small, w) in enumerate(
            (("band", "mesh", width),) + (("band", "mesh", half),) * 2 + (("mesh", "band", half),) * 2
        )
    ]
    sum_u, sum_g = (sum_u0, sum_u1), (sum_g0, sum_g1)

    def send_slopes(c):
        s_in[c, me] = s_part[c, me]
        return send_all("mesh", nm, lambda p: s_part.at[c, p], lambda q: s_in.at[c, q], ss.at[c], rs.at[c])

    enter((("mesh", nm), ("band", nb)))
    sent_a = send_all("mesh", nm, lambda p: a_part.at[p], lambda q: a_in.at[q], sa, ra)
    sent_s = [send_slopes(0)]
    a_in[me] = a_part[me]
    own = dot(ml[...], w_self[...]) + b_node[...]
    back = dot_nt(ct[...], w_node[...])

    def build(b, carry):
        cut = pl.ds(pl.multiple_of(b * EB, EB), EB)
        per = EB // 128
        hot = jnp.concatenate(
            [onehot(grid_rows[pl.ds(b * per + u, 1), :] == iota((grid_dev, 128), 0)) for u in range(per)],
            axis=1,
        )
        lat_e[:, cut] = dot(latent_t[...], hot).astype(BF16)
        scol = slot_col[cut, :]
        for t in range(slots_n // 128):
            hot_s[cut, t * 128 : (t + 1) * 128] = onehot(scol == iota((EB, 128), 1) + t * 128)
        return carry

    lax.fori_loop(0, rows * 128 // EB, build, 0)
    rows_t[...] = jnp.transpose(rows_in[...].astype(F32)).astype(BF16)
    wait_all(sent_a)
    acts = dot_tn(pick[...], a_in[...].reshape(flat, width))[0:mesh_dev].astype(BF16)
    agg = dot(acts, w_edge[...]).astype(BF16)
    node_pre = own + dot(agg, w_agg[...])
    s = sigmoid(node_pre)
    node_act = node_pre * s
    g_node = (back * (s + node_act * (1.0 - s))).astype(BF16)
    g_agg = dot_nt(g_node, w_agg[...]).astype(BF16)
    h = dot_nt(g_agg, w_edge[...])
    hb = jnp.concatenate(
        [h.astype(BF16), jnp.zeros((pick.shape[1] - mesh_dev, width), BF16)], axis=0
    )
    sent_h = []
    for c in range(2):
        asked[c] = dot(pick[...], hb[:, c * half : (c + 1) * half]).astype(BF16).reshape(nm, CAP, half)
        sent_h.append(send_all("mesh", nm, lambda p, c=c: asked.at[c, p], lambda q, c=c: landed.at[c, q],
                               sh.at[c], rh.at[c]))
        landed[c, me] = asked[c, me]
    ge[...] = dot_tn(acts, g_agg).astype(BF16)
    sum_e[0](ge)
    mesh_out[...] = (ml[...].astype(F32) + dot(node_act.astype(BF16), w_node[...])).astype(BF16)
    part = ct[...].astype(F32) + dot_nt(g_node, w_self[...])

    def halves(c):
        acc[...] = jnp.zeros_like(acc)
        col = slice(c * half, (c + 1) * half)

        def block(b, carry):
            cut = pl.ds(pl.multiple_of(b * GB, GB), GB)
            g = (dot(hot_s[cut, :], table) * slope[cut, col].astype(F32)).astype(BF16)
            acc[...] += dot(lat_e[:, cut], g)
            return carry

        wait_all(sent_h[c])
        table = landed[c].reshape(flat, half)
        lax.fori_loop(0, rows * 128 // GB, block, 0)
        gg[c] = acc[...].astype(BF16)
        sum_g[c][0](gg.at[c])
        pm = (table.astype(F32) * s_part[c].reshape(flat, half).astype(F32)).astype(BF16)
        gu[c] = dot(rows_t[...], pm).astype(BF16)
        sum_u[c][0](gu.at[c])

    halves(0)
    sum_e[1]()
    halves(1)
    sent_s.append(send_slopes(1))
    sum_g0[1]()
    sum_u0[1]()
    sum_e[2]()
    sum_g1[1]()
    sum_u1[1]()
    sum_g0[2]()
    sum_u0[2]()
    sum_e[3]()
    sum_g1[2]()
    sum_u1[2]()
    sum_u0[3]()
    wait_all(sent_s[0])
    wait_all(sent_s[1])
    slopes = jnp.concatenate(
        [dot_tn(pick[...], s_in[c].reshape(flat, half))[0:mesh_dev] for c in range(2)], axis=1
    )
    g_pmesh = (h * slopes).astype(BF16)
    sum_u1[3]()
    grad_mesh[...] = (part + dot_nt(g_pmesh, u_mesh[...])).astype(BF16)
    sum_e[4](oe)
    sum_g0[4](og0)
    sum_u0[4](ou0)
    sum_g1[4](og1)
    sum_u1[4](ou1)


def write_kernel(mo, gm, e, u0, u1, g0, g1, mo_out, gm_out, e_out, g_out, u_out):
    half = g0.shape[1]
    mo_out[...] = mo[...]
    gm_out[...] = gm[...]
    e_out[...] = e[...].astype(F32)
    u_out[:, 0:half] = u0[...].astype(F32)
    u_out[:, half:] = u1[...].astype(F32)
    g_out[:, 0:half] = g0[...].astype(F32)
    g_out[:, half:] = g1[...].astype(F32)


def vmem():
    return pl.BlockSpec(memory_space=pltpu.VMEM)


def shape(dims, kind):
    return jax.ShapeDtypeStruct(dims, kind)


def params(mib, cid=None):
    if cid is None:
        return pltpu.CompilerParams(vmem_limit_bytes=mib * MIB)
    return pltpu.CompilerParams(
        vmem_limit_bytes=mib * MIB, collective_id=cid, has_side_effects=True
    )


def shards(
    nb, nm, grid_vars, mesh_latent, cotangent, edge_grid, edge_mesh, w_in, b_in, w_out, norm_gain,
    u_grid, u_mesh, b_edge, w_edge, w_self, w_agg, b_node, w_node_out,
):
    grid_dev = grid_vars.shape[0]
    mesh_dev, width = mesh_latent.shape
    edges = edge_grid.shape[0]
    rows = edges // 128
    slots_n = nm * CAP
    padded = -(-mesh_dev // 128) * 128
    sem = pltpu.SemaphoreType.DMA
    em = edge_mesh.reshape(rows, 128)
    eg = edge_grid.reshape(rows, 128)
    table, rows_in, pick, latent_t, pre_grid, slots, slot_col, local_grid = pl.pallas_call(
        functools.partial(fetch_kernel, nb, nm),
        out_shape=(
            shape((slots_n, width), BF16), shape((slots_n, width), BF16), shape((slots_n, padded), BF16),
            shape((width, grid_dev), BF16), shape((edges, width), BF16),
            shape((rows, 128), jnp.int32), shape((edges, 128), jnp.int32), shape((rows, 128), jnp.int32),
        ),
        in_specs=[vmem()] * 10,
        out_specs=(vmem(),) * 8,
        scratch_shapes=[
            pltpu.VMEM((edges, 128), jnp.int32), pltpu.VMEM((grid_dev, width), BF16),
            pltpu.VMEM((2 * nm, edges), BF16), pltpu.VMEM((128, edges), BF16),
            pltpu.VMEM((nm, 8, 128), F32), pltpu.VMEM((nm, 8, 128), F32),
            pltpu.VMEM((nm, CAP, width), BF16), pltpu.VMEM((nm, CAP, width), BF16),
            pltpu.VMEM((padded, width), BF16),
            sem((nm,)), sem((nm,)), sem((nm,)), sem((nm,)),
        ],
        compiler_params=params(20, 0),
        name="fetch",
    )(em, eg, grid_vars.T, mesh_latent, w_in, b_in.reshape(1, -1), w_out, norm_gain.reshape(1, -1),
      u_grid, u_mesh)
    half = width // 2
    a_part, s_part, slope = pl.pallas_call(
        edge_kernel,
        out_shape=(
            shape((slots_n, width), BF16), shape((2, slots_n, half), BF16), shape((edges, width), BF16),
        ),
        in_specs=[pl.BlockSpec(memory_space=pltpu.SMEM)] + [vmem()] * 5,
        out_specs=(vmem(),) * 3,
        scratch_shapes=[
            pltpu.VMEM((slots_n, 2 * width), F32), pltpu.VMEM((EB, width), F32),
            pltpu.VMEM((EB, 2 * width), BF16),
        ],
        compiler_params=params(16),
        name="edges",
    )(slots, slots, slot_col, table, pre_grid, b_edge.reshape(1, -1))
    sums = []
    for n, m, w in ((nb, nm, width), (nb, nm, half), (nb, nm, half), (nm, nb, half), (nm, nb, half)):
        big = width // n
        if n == nm:
            mid = [pltpu.VMEM((big, w), BF16), pltpu.VMEM((m, big, w), BF16), pltpu.VMEM((8, 128), F32)]
        else:
            across = min(m, w // 128)
            piece = pltpu.VMEM((m, big // (m // across), w // across), F32)
            mid = [piece] * 3
        sums += [pltpu.VMEM((n, big, w), BF16)] + mid + [
            pltpu.VMEM((n, big, w), BF16), sem((2, n)), sem((2, m)), sem((2, m)), sem((2, n)),
        ]
    scale = (edges * nb * nm) ** (-0.5)
    node = shape((mesh_dev, width), BF16)
    slim = shape((width, half), BF16)
    blocks = pltpu.VMEM((2, nm, CAP, half), BF16)
    outs = pl.pallas_call(
        functools.partial(back_kernel, nb, nm, scale),
        out_shape=(node, node, shape((width, width), BF16), slim, slim, slim, slim),
        in_specs=[vmem()] * 16,
        out_specs=(vmem(),) * 7,
        scratch_shapes=[
            pltpu.VMEM((nm, CAP, width), BF16), blocks, blocks, blocks,
            pltpu.VMEM((edges, slots_n), BF16), pltpu.VMEM((width, edges), BF16),
            pltpu.VMEM((width, slots_n), BF16), pltpu.VMEM((width, half), F32),
            pltpu.VMEM((width, width), BF16), pltpu.VMEM((2, width, half), BF16),
            pltpu.VMEM((2, width, half), BF16),
            sem((nm,)), sem((nm,)), sem((2, nm)), sem((2, nm)), sem((2, nm)), sem((2, nm)),
        ] + sums,
        compiler_params=params(38, 1),
        name="back",
    )(pick, mesh_latent, cotangent, b_node.reshape(1, -1), local_grid, a_part.reshape(nm, CAP, width),
      s_part.reshape(2, nm, CAP, half), w_edge, w_self, w_agg, w_node_out, u_mesh, slot_col, slope, latent_t,
      rows_in)
    final = shape((width, width), F32)
    return pl.pallas_call(
        write_kernel,
        out_shape=(node, node, final, final, final),
        in_specs=[vmem()] * 7,
        out_specs=(vmem(),) * 5,
        compiler_params=params(16),
        name="write",
    )(*outs)


def solution(mesh):
    split = P(("band", "mesh"), None)
    flat = P(("band", "mesh"))
    return jax.shard_map(
        functools.partial(shards, mesh.shape["band"], mesh.shape["mesh"]),
        mesh=mesh,
        in_specs=(split, split, split, flat, flat) + (P(),) * 12,
        out_specs=(split, split, P(), P(), P()),
        check_vma=False,
    )
```

time: 135 us -> 121 us (0.90)
  Pallas kernels: 134 us -> 110 us
  local copies, waits for them, and re-layouts: 0 us -> 9.73 us
    pallas_call x1, Pallas kernels: 82.4 us -> 72.4 us  [shards(): pl.pallas_call(functools.partial(back_kernel, nb, nm, scale), out_shape=(...]
    unnamed x0 -> x38, local copies, waits for them, and re-layouts: none -> 9.73 us
    pallas_call x1, Pallas kernels: 21.6 us -> 12.1 us  [shards(): pl.pallas_call(edge_kernel, out_shape=(shape((slots_n, width), BF16), sha...]
    pallas_call x1, Pallas kernels: 26.6 us -> 23.4 us  [shards(): pl.pallas_call(functools.partial(fetch_kernel, nb, nm), out_shape=(shape(...]
    pallas_call x1, Pallas kernels: 3.44 us -> 2.08 us  [shards(): pl.pallas_call(write_kernel, out_shape=(node, node, final, final, final),...]
where the time goes in v3:
time: 121 us
  Pallas kernels  110 us (91%)
  local copies, waits for them, and re-layouts  9.73 us (8%)
    pallas_call x1, Pallas kernels, shards(): pl.pallas_call(functools.partial(back_kernel, nb, nm, scale), out_shape=(...  72.4 us
    pallas_call x1, Pallas kernels, shards(): pl.pallas_call(functools.partial(fetch_kernel, nb, nm), out_shape=(shape(...  23.4 us
    pallas_call x1, Pallas kernels, shards(): pl.pallas_call(edge_kernel, out_shape=(shape((slots_n, width), BF16), sha...  12.1 us
    unnamed x38, local copies, waits for them, and re-layouts  9.73 us

profile of v3, /device:TPU:1, one launch (start us, length us, event | category | flops | bytes accessed | tf_op | source)
XLA Modules:
  0.0 120.5 jit_solution(10517854741881461339)
XLA Ops:
  0.6 0.0 copy-start
  0.6 1.0 copy-done
  1.7 1.0 copy-done.2
  2.7 1.0 copy-done.8
  3.7 1.0 copy-done.9
  4.7 1.0 copy-done.10
  5.8 0.9 copy-done.12
  6.7 0.7 copy-done.13
  7.4 0.7 copy-done.14
  8.1 0.7 copy-done.15
  8.8 0.7 copy-done.16
  9.5 23.4 %fetch.1 = (bf16[768,512]{1,0:T(8,128)(2,1)S(1)}, bf16[768,512]{1,0:T(8,128)(2,1)S(1)}, bf16[768,384]{1,0:T(8,128)(2,1)S(1)}, bf16[512,1024]{1,0:T(8,128)(2,1)S(...) custom-call(s32[32,128]{1,0:T(8,128)S(1)} %bitcast.12, ...), custom_call_target="tpu_custom_call" | custom-call | tf_op jit(solution)/shard_map/fetch/pallas_call | solution.py:471
  32.9 0.0 copy-start.1
  32.9 0.0 copy-start.3
  32.9 0.0 copy-start.4
  32.9 0.0 copy-start.5
  32.9 0.0 copy-start.6
  32.9 0.0 copy-start.7
  33.0 0.0 copy-start.11
  33.0 0.0 copy-start.17
  33.0 0.8 copy-done.17
  33.8 12.1 %edges.1 = (bf16[768,512]{1,0:T(8,128)(2,1)S(1)}, bf16[2,768,256]{2,1,0:T(8,128)(2,1)S(1)}, bf16[4096,512]{1,0:T(8,128)(2,1)S(1)}) custom-call(s32[32,128]{1,0:T(8,128)S(1)} %get-tuple-element.25.slot_s.slots, s32[32,128]{1,0:T(8,128)S(1)} %get-tuple-element.25.slot_s.slots, s32[4096,128]{1,0:T(8,128)S(1)} %get-tuple-element.26.slot_col, ...), custom_call_target="tpu_custom_call" | custom-call | tf_op jit(solution)/shard_map/edges/pallas_call | solution.py:493
  45.9 0.0 copy-done.18
  45.9 0.0 copy-done.1
  45.9 0.0 copy-done.3
  46.0 0.0 copy-done.4
  46.0 0.0 copy-done.5
  46.0 0.0 copy-done.6
  46.0 0.0 copy-done.7
  46.0 0.0 copy-done.11
  46.0 72.4 %back.1 = (bf16[320,512]{1,0:T(8,128)(2,1)S(1)}, bf16[320,512]{1,0:T(8,128)(2,1)S(1)}, bf16[512,512]{1,0:T(8,128)(2,1)S(1)}, bf16[512,256]{1,0:T(8,128)(2,1)S(1)...) custom-call(bf16[768,384]{1,0:T(8,128)(2,1)S(1)} %get-tuple-element.23.pick, ...), custom_call_target="tpu_custom_call" | custom-call | tf_op jit(solution)/shard_map/back/pallas_call | solution.py:523
  118.4 2.1 %write.1 = (bf16[320,512]{1,0:T(8,128)(2,1)}, bf16[320,512]{1,0:T(8,128)(2,1)}, f32[512,512]{1,0:T(8,128)}, f32[512,512]{1,0:T(8,128)}, f32[512,512]{1,0:T(8,128)}) custom-call(bf16[320,512]{1,0:T(8,128)(2,1)S(1)} %get-tuple-element.34.mo, bf16[320,512]{1,0:T(8,128)(2,1)S(1)} %get-tuple-element.35.gm, bf16[512,512]{1,0:T(8,128)(2,1)S(1)} %get-tuple-element.36.e, ...), custom_call_target="tpu_custom_call" | custom-call | tf_op jit(solution)/shard_map/write/pallas_call | solution.py:542
  (10 shorter events, 0.0 us)
Async XLA Ops:
  0.6 1.0 copy-start
  1.7 1.0 copy-start.2
  2.7 1.0 copy-start.8
  3.7 1.0 copy-start.9
  4.7 1.0 copy-start.10
  5.8 0.9 copy-start.12
  6.7 0.7 copy-start.13
  7.4 0.7 copy-start.14
  8.1 0.7 copy-start.15
  8.8 0.7 copy-start.16
  9.5 36.4 %copy-start.18 = (f32[512]{0:T(512)S(1)}, f32[512]{0:T(512)}, u32[]{:S(2)}) copy-start(f32[512]{0:T(512)} %param.32) | copy-start | bytes 6148
  32.9 13.1 %copy-start.1 = (bf16[512,512]{1,0:T(8,128)(2,1)S(1)}, bf16[512,512]{1,0:T(8,128)(2,1)}, u32[]{:S(2)}) copy-start(bf16[512,512]{1,0:T(8,128)(2,1)} %u_mesh.3) | copy-start | bytes 1572868
  32.9 13.1 %copy-start.3 = (bf16[320,512]{1,0:T(8,128)(2,1)S(1)}, bf16[320,512]{1,0:T(8,128)(2,1)}, u32[]{:S(2)}) copy-start(bf16[320,512]{1,0:T(8,128)(2,1)} %ml.3) | copy-start | bytes 983044
  32.9 13.1 %copy-start.4 = (bf16[512,512]{1,0:T(8,128)(2,1)S(1)}, bf16[512,512]{1,0:T(8,128)(2,1)}, u32[]{:S(2)}) copy-start(bf16[512,512]{1,0:T(8,128)(2,1)} %w_edge.1) | copy-start | bytes 1572868
  32.9 13.0 %copy-start.5 = (bf16[512,512]{1,0:T(8,128)(2,1)S(1)}, bf16[512,512]{1,0:T(8,128)(2,1)}, u32[]{:S(2)}) copy-start(bf16[512,512]{1,0:T(8,128)(2,1)} %w_self.1) | copy-start | bytes 1572868
  32.9 13.0 %copy-start.6 = (bf16[512,512]{1,0:T(8,128)(2,1)S(1)}, bf16[512,512]{1,0:T(8,128)(2,1)}, u32[]{:S(2)}) copy-start(bf16[512,512]{1,0:T(8,128)(2,1)} %w_agg.1) | copy-start | bytes 1572868
  32.9 13.0 %copy-start.7 = (bf16[512,512]{1,0:T(8,128)(2,1)S(1)}, bf16[512,512]{1,0:T(8,128)(2,1)}, u32[]{:S(2)}) copy-start(bf16[512,512]{1,0:T(8,128)(2,1)} %w_node.1) | copy-start | bytes 1572868
  33.0 13.0 %copy-start.11 = (bf16[320,512]{1,0:T(8,128)(2,1)S(1)}, bf16[320,512]{1,0:T(8,128)(2,1)}, u32[]{:S(2)}) copy-start(bf16[320,512]{1,0:T(8,128)(2,1)} %ct.1) | copy-start | bytes 983044
  33.0 0.8 copy-start.17

commit v4 on v3

--- a/solution.py
+++ b/solution.py
@@ -42,17 +42,18 @@
     return jnp.where(mask, 1.0, 0.0).astype(BF16)
 
 
-def enter(axes):
+def greet(axes):
     barrier = pltpu.get_barrier_semaphore()
-    total = 0
     for axis, n in axes:
         me = lax.axis_index(axis)
         for d in range(1, n):
             pl.semaphore_signal(
                 barrier, inc=1, device_id={axis: lax.rem(me + d, n)}, device_id_type=MESH
             )
-        total += n - 1
-    pl.semaphore_wait(barrier, total)
+
+
+def gathered(axes):
+    pl.semaphore_wait(pltpu.get_barrier_semaphore(), sum(n - 1 for _, n in axes))
 
 
 def send_all(axis, n, src, dst, send_sem, recv_sem):
@@ -90,16 +91,26 @@
 
 
 def fetch_kernel(
-    nb, nm, em, eg, gv, ml, w_in, b_in, w_out, gain, u_grid, u_mesh,
-    table, rows_in, pick, latent_t, pre_grid, slots, slot_col, local_grid,
-    grid_col, pgrid, left, right, ids_out, ids_in, asked, landed, padded, s1, r1, s2, r2,
+    nb, nm, em_h, eg_h, gv_h, ml_h, w_in_h, b_in_h, w_out_h, gain_h, u_grid_h, u_mesh_h, b_edge_h,
+    table, rows_in, pick, latent_t, pre_grid, slots, slot_col, local_grid, b_edge,
+    em, eg, gv, ml, w_in, b_in, w_out, gain, u_grid, u_mesh, load_sem, grid_col, pgrid, left, right, ids_out, ids_in, asked, landed, padded, s1, r1, s2, r2,
 ):
     mesh_dev = ml.shape[0]
     grid_dev = gv.shape[1]
     rows = em.shape[0]
     me = lax.axis_index("mesh")
     band = lax.axis_index("band")
-    enter((("mesh", nm),))
+    loads = []
+    for i, (src, dst) in enumerate(
+        ((em_h, em), (eg_h, eg), (ml_h, ml), (gv_h, gv), (w_in_h, w_in), (b_in_h, b_in), (w_out_h, w_out),
+         (gain_h, gain), (u_grid_h, u_grid), (u_mesh_h, u_mesh), (b_edge_h, b_edge))
+    ):
+        copy = pltpu.make_async_copy(src, dst, load_sem.at[i])
+        copy.start()
+        loads.append(copy)
+    everyone = (("mesh", nm),)
+    greet(everyone)
+    loads[0].wait()
     x = em[...] - band * (nm * mesh_dev)
     lane = iota(x.shape, 1)
     row = iota(x.shape, 0)
@@ -137,8 +148,11 @@
     ids = both[0:nm] * 16.0 + both[nm : 2 * nm]
     for o in range(nm):
         ids_out[o] = jnp.broadcast_to(ids[o : o + 1, :], (8, 128))
+    gathered(everyone)
     sent = send_all("mesh", nm, lambda p: ids_out.at[p], lambda q: ids_in.at[q], s1, r1)
     ids_in[me] = ids_out[me]
+    for copy in loads[1:3]:
+        copy.wait()
     padded[0:mesh_dev, :] = ml[...]
     padded[mesh_dev:, :] = jnp.zeros((padded.shape[0] - mesh_dev, padded.shape[1]), BF16)
     columns(slots, slot_col)
@@ -155,6 +169,8 @@
     asked[...] = dot(pick[...], padded[...]).astype(BF16).reshape(asked.shape)
     sent = send_all("mesh", nm, lambda p: asked.at[p], lambda q: landed.at[q], s2, r2)
     landed[me] = asked[me]
+    for copy in loads[3:]:
+        copy.wait()
     step = 256
 
     def grid_rows(i, carry):
@@ -193,36 +209,61 @@
     per = EB // 128
     acc[...] = jnp.zeros_like(acc)
 
+    def finish(v):
+        s = sigmoid(v)
+        act = v * s
+        return act.astype(BF16), (s + act * (1.0 - s)).astype(BF16)
+
     def block(b, carry):
         cut = pl.ds(pl.multiple_of(b * EB, EB), EB)
-        pre[...] = pre_grid[cut, :].astype(F32) + b_edge[...]
         low = slot_s[b * per, 0]
         high = slot_s[b * per + per - 1, 127]
-        for t in range(tiles):
-            @pl.when((low < (t + 1) * TB) & (high >= t * TB))
-            def _():
-                scol = slot_col[cut, :]
-                hot = jnp.concatenate(
-                    [onehot(scol == iota((EB, 128), 1) + (t * TB + u * 128)) for u in range(TB // 128)],
-                    axis=1,
-                )
-                pre[...] += dot(hot, table[t * TB : (t + 1) * TB, :])
-
-        v = pre[...]
-        s = sigmoid(v)
-        act = v * s
-        both[:, 0:width] = act.astype(BF16)
-        sl = (s + act * (1.0 - s)).astype(BF16)
-        both[:, width:] = sl
-        slope[cut, :] = sl
-        for t in range(tiles):
-            @pl.when((low < (t + 1) * TB) & (high >= t * TB))
-            def _():
-                hot = jnp.concatenate(
-                    [onehot(slots[pl.ds(b * per + u, 1), :] == iota((TB, 128), 0) + t * TB) for u in range(per)],
-                    axis=1,
-                )
-                acc[t * TB : (t + 1) * TB, :] += dot(hot, both[...])
+        base = pl.multiple_of(jnp.right_shift(low, TB.bit_length() - 1) * TB, TB)
+        single = high < base + TB
+
+        @pl.when(single)
+        def _():
+            window = table[pl.ds(base, TB), :]
+            for u in range(per):
+                part = pl.ds(pl.multiple_of(b * EB + u * 128, 128), 128)
+                scol = slot_col[part, :] - base
+                hot = jnp.concatenate([onehot(scol == iota((128, 128), 1) + w * 128) for w in range(TB // 128)], axis=1)
+                v = pre_grid[part, :].astype(F32) + b_edge[...] + dot(hot, window)
+                act, sl = finish(v)
+                both[u * 128 : (u + 1) * 128, 0:width] = act
+                both[u * 128 : (u + 1) * 128, width:] = sl
+                slope[part, :] = sl
+            hot = jnp.concatenate(
+                [onehot(slots[pl.ds(b * per + u, 1), :] - base == iota((TB, 128), 0)) for u in range(per)],
+                axis=1,
+            )
+            acc[pl.ds(base, TB), :] += dot(hot, both[...])
+
+        @pl.when(jnp.logical_not(single))
+        def _():
+            pre[...] = pre_grid[cut, :].astype(F32) + b_edge[...]
+            for t in range(tiles):
+                @pl.when((low < (t + 1) * TB) & (high >= t * TB))
+                def _():
+                    scol = slot_col[cut, :]
+                    hot = jnp.concatenate(
+                        [onehot(scol == iota((EB, 128), 1) + (t * TB + u * 128)) for u in range(TB // 128)],
+                        axis=1,
+                    )
+                    pre[...] += dot(hot, table[t * TB : (t + 1) * TB, :])
+
+            act, sl = finish(pre[...])
+            both[:, 0:width] = act
+            both[:, width:] = sl
+            slope[cut, :] = sl
+            for t in range(tiles):
+                @pl.when((low < (t + 1) * TB) & (high >= t * TB))
+                def _():
+                    hot = jnp.concatenate(
+                        [onehot(slots[pl.ds(b * per + u, 1), :] == iota((TB, 128), 0) + t * TB) for u in range(per)],
+                        axis=1,
+                    )
+                    acc[t * TB : (t + 1) * TB, :] += dot(hot, both[...])
 
         return carry
 
@@ -233,7 +274,7 @@
         s_out[c] = acc[:, width + c * half : width + (c + 1) * half].astype(BF16)
 
 
-def make_sum(axes, scale, big, small, width, in1, mid, in2, all2, all1, q1, q2, q3, q4):
+def make_sum(axes, scale, big, small, width, all1, in1, mid, in2, all2, q1, q2, q3, q4):
     n, m = axes[big], axes[small]
     rows = in1.shape[1]
     live = {}
@@ -257,9 +298,8 @@
         all1[me] = values.astype(BF16)
         live[4] = send_all(big, n, lambda p: all1.at[me], lambda q: all1.at[q], q4.at[0], q4.at[1])
 
-    def finish(out):
+    def finish():
         wait_all(live[4])
-        out[...] = all1[...].reshape(out.shape)
 
     if small == "band":
 
@@ -323,7 +363,7 @@
     me = lax.axis_index("mesh")
     axes = {"band": nb, "mesh": nm}
     sum_e, sum_u0, sum_u1, sum_g0, sum_g1 = [
-        make_sum(axes, scale, big, small, w, *sums[i * 9 : (i + 1) * 9])
+        make_sum(axes, scale, big, small, w, (oe, ou0, ou1, og0, og1)[i], *sums[i * 8 : (i + 1) * 8])
         for i, (big, small, w) in enumerate(
             (("band", "mesh", width),) + (("band", "mesh", half),) * 2 + (("mesh", "band", half),) * 2
         )
@@ -334,7 +374,9 @@
         s_in[c, me] = s_part[c, me]
         return send_all("mesh", nm, lambda p: s_part.at[c, p], lambda q: s_in.at[c, q], ss.at[c], rs.at[c])
 
-    enter((("mesh", nm), ("band", nb)))
+    everyone = (("mesh", nm), ("band", nb))
+    greet(everyone)
+    gathered(everyone)
     sent_a = send_all("mesh", nm, lambda p: a_part.at[p], lambda q: a_in.at[q], sa, ra)
     sent_s = [send_slopes(0)]
     a_in[me] = a_part[me]
@@ -374,58 +416,55 @@
         sent_h.append(send_all("mesh", nm, lambda p, c=c: asked.at[c, p], lambda q, c=c: landed.at[c, q],
                                sh.at[c], rh.at[c]))
         landed[c, me] = asked[c, me]
+    sent_s.append(send_slopes(1))
     ge[...] = dot_tn(acts, g_agg).astype(BF16)
     sum_e[0](ge)
     mesh_out[...] = (ml[...].astype(F32) + dot(node_act.astype(BF16), w_node[...])).astype(BF16)
     part = ct[...].astype(F32) + dot_nt(g_node, w_self[...])
 
-    def halves(c):
+    def halves(c, between):
         acc[...] = jnp.zeros_like(acc)
         col = slice(c * half, (c + 1) * half)
-
-        def block(b, carry):
-            cut = pl.ds(pl.multiple_of(b * GB, GB), GB)
-            g = (dot(hot_s[cut, :], table) * slope[cut, col].astype(F32)).astype(BF16)
-            acc[...] += dot(lat_e[:, cut], g)
-            return carry
-
         wait_all(sent_h[c])
         table = landed[c].reshape(flat, half)
-        lax.fori_loop(0, rows * 128 // GB, block, 0)
-        gg[c] = acc[...].astype(BF16)
-        sum_g[c][0](gg.at[c])
         pm = (table.astype(F32) * s_part[c].reshape(flat, half).astype(F32)).astype(BF16)
         gu[c] = dot(rows_t[...], pm).astype(BF16)
         sum_u[c][0](gu.at[c])
-
-    halves(0)
-    sum_e[1]()
-    halves(1)
-    sent_s.append(send_slopes(1))
+        for b in range(rows * 128 // GB):
+            cut = slice(b * GB, (b + 1) * GB)
+            g = (dot(hot_s[cut, :], table) * slope[cut, col].astype(F32)).astype(BF16)
+            acc[...] += dot(lat_e[:, cut], g)
+            if b in between:
+                between[b]()
+        gg[c] = acc[...].astype(BF16)
+        sum_g[c][0](gg.at[c])
+
+    last = rows * 128 // GB - 1
+    halves(0, {min(1, last): sum_e[1]})
+    halves(1, {0: sum_u0[1]})
+    sum_e[2]()
+    sum_u1[1]()
+    sum_u0[2]()
     sum_g0[1]()
-    sum_u0[1]()
-    sum_e[2]()
-    sum_g1[1]()
-    sum_u1[1]()
-    sum_g0[2]()
-    sum_u0[2]()
-    sum_e[3]()
-    sum_g1[2]()
-    sum_u1[2]()
-    sum_u0[3]()
     wait_all(sent_s[0])
     wait_all(sent_s[1])
     slopes = jnp.concatenate(
         [dot_tn(pick[...], s_in[c].reshape(flat, half))[0:mesh_dev] for c in range(2)], axis=1
     )
     g_pmesh = (h * slopes).astype(BF16)
+    grad_mesh[...] = (part + dot_nt(g_pmesh, u_mesh[...])).astype(BF16)
+    sum_e[3]()
+    sum_g0[2]()
+    sum_u0[3]()
+    sum_g1[1]()
+    sum_u1[2]()
+    sum_g1[2]()
     sum_u1[3]()
-    grad_mesh[...] = (part + dot_nt(g_pmesh, u_mesh[...])).astype(BF16)
-    sum_e[4](oe)
-    sum_g0[4](og0)
-    sum_u0[4](ou0)
-    sum_g1[4](og1)
-    sum_u1[4](ou1)
+    sum_e[4]()
+    sum_g0[4]()
+    sum_u0[4]()
+    sum_u1[4]()
+    sum_g1[4]()
 
 
 def write_kernel(mo, gm, e, u0, u1, g0, g1, mo_out, gm_out, e_out, g_out, u_out):
@@ -468,16 +507,22 @@
     sem = pltpu.SemaphoreType.DMA
     em = edge_mesh.reshape(rows, 128)
     eg = edge_grid.reshape(rows, 128)
-    table, rows_in, pick, latent_t, pre_grid, slots, slot_col, local_grid = pl.pallas_call(
+    table, rows_in, pick, latent_t, pre_grid, slots, slot_col, local_grid, bias = pl.pallas_call(
         functools.partial(fetch_kernel, nb, nm),
         out_shape=(
             shape((slots_n, width), BF16), shape((slots_n, width), BF16), shape((slots_n, padded), BF16),
             shape((width, grid_dev), BF16), shape((edges, width), BF16),
             shape((rows, 128), jnp.int32), shape((edges, 128), jnp.int32), shape((rows, 128), jnp.int32),
+            shape((1, width), F32),
         ),
-        in_specs=[vmem()] * 10,
-        out_specs=(vmem(),) * 8,
+        in_specs=[pl.BlockSpec(memory_space=pltpu.HBM)] * 11,
+        out_specs=(vmem(),) * 9,
         scratch_shapes=[
+            pltpu.VMEM((rows, 128), jnp.int32), pltpu.VMEM((rows, 128), jnp.int32),
+            pltpu.VMEM((grid_vars.shape[1], grid_dev), BF16), pltpu.VMEM((mesh_dev, width), BF16),
+            pltpu.VMEM((grid_vars.shape[1], width), BF16), pltpu.VMEM((1, width), F32),
+            pltpu.VMEM((width, width), BF16), pltpu.VMEM((1, width), F32),
+            pltpu.VMEM((width, width), BF16), pltpu.VMEM((width, width), BF16), sem((11,)),
             pltpu.VMEM((edges, 128), jnp.int32), pltpu.VMEM((grid_dev, width), BF16),
             pltpu.VMEM((2 * nm, edges), BF16), pltpu.VMEM((128, edges), BF16),
             pltpu.VMEM((nm, 8, 128), F32), pltpu.VMEM((nm, 8, 128), F32),
@@ -485,10 +530,13 @@
             pltpu.VMEM((padded, width), BF16),
             sem((nm,)), sem((nm,)), sem((nm,)), sem((nm,)),
         ],
-        compiler_params=params(20, 0),
+        compiler_params=params(24, 0),
         name="fetch",
-    )(em, eg, grid_vars.T, mesh_latent, w_in, b_in.reshape(1, -1), w_out, norm_gain.reshape(1, -1),
-      u_grid, u_mesh)
+    )(*[
+        pltpu.with_memory_space_constraint(v, pltpu.HBM)
+        for v in (em, eg, grid_vars.T, mesh_latent, w_in, b_in.reshape(1, -1), w_out,
+                  norm_gain.reshape(1, -1), u_grid, u_mesh, b_edge.reshape(1, -1))
+    ])
     half = width // 2
     a_part, s_part, slope = pl.pallas_call(
         edge_kernel,
@@ -503,7 +551,7 @@
         ],
         compiler_params=params(16),
         name="edges",
-    )(slots, slots, slot_col, table, pre_grid, b_edge.reshape(1, -1))
+    )(slots, slots, slot_col, table, pre_grid, bias)
     sums = []
     for n, m, w in ((nb, nm, width), (nb, nm, half), (nb, nm, half), (nm, nb, half), (nm, nb, half)):
         big = width // n
@@ -514,15 +562,16 @@
             piece = pltpu.VMEM((m, big // (m // across), w // across), F32)
             mid = [piece] * 3
         sums += [pltpu.VMEM((n, big, w), BF16)] + mid + [
-            pltpu.VMEM((n, big, w), BF16), sem((2, n)), sem((2, m)), sem((2, m)), sem((2, n)),
+            sem((2, n)), sem((2, m)), sem((2, m)), sem((2, n)),
         ]
     scale = (edges * nb * nm) ** (-0.5)
     node = shape((mesh_dev, width), BF16)
-    slim = shape((width, half), BF16)
+    slim_u = shape((nb, width // nb, half), BF16)
+    slim_g = shape((nm, width // nm, half), BF16)
     blocks = pltpu.VMEM((2, nm, CAP, half), BF16)
     outs = pl.pallas_call(
         functools.partial(back_kernel, nb, nm, scale),
-        out_shape=(node, node, shape((width, width), BF16), slim, slim, slim, slim),
+        out_shape=(node, node, shape((nb, width // nb, width), BF16), slim_u, slim_u, slim_g, slim_g),
         in_specs=[vmem()] * 16,
         out_specs=(vmem(),) * 7,
         scratch_shapes=[
@@ -546,7 +595,7 @@
         out_specs=(vmem(),) * 5,
         compiler_params=params(16),
         name="write",
-    )(*outs)
+    )(*outs[:2], *[o.reshape(width, o.shape[2]) for o in outs[2:]])
 
 
 def solution(mesh):

time: 121 us -> 110 us (0.909)
  local copies, waits for them, and re-layouts: 9.73 us -> 0.05 us
    unnamed x38 -> x16, local copies, waits for them, and re-layouts: 9.73 us -> 0.05 us
where the time goes in v4:
time: 110 us
  Pallas kernels  109 us (99%)
    pallas_call x1, Pallas kernels, shards(): pl.pallas_call(functools.partial(back_kernel, nb, nm, scale), out_shape=(...  73.3 us
    pallas_call x1, Pallas kernels, shards(): pl.pallas_call(functools.partial(fetch_kernel, nb, nm), out_shape=(shape(...  22.5 us
    pallas_call x1, Pallas kernels, shards(): pl.pallas_call(edge_kernel, out_shape=(shape((slots_n, width), BF16), sha...  11 us

profile of v4, /device:TPU:1, one launch (start us, length us, event | category | flops | bytes accessed | tf_op | source)
XLA Modules:
  0.0 109.8 jit_solution(6757022399934889167)
XLA Ops:
  0.6 22.5 %fetch.1 = (bf16[768,512]{1,0:T(8,128)(2,1)S(1)}, bf16[768,512]{1,0:T(8,128)(2,1)S(1)}, bf16[768,384]{1,0:T(8,128)(2,1)S(1)}, bf16[512,1024]{1,0:T(8,128)(2,1)S(...) custom-call(s32[32,128]{1,0:T(8,128)} %bitcast.23, ...), custom_call_target="tpu_custom_call" | custom-call | tf_op jit(solution)/shard_map/fetch/pallas_call | solution.py:510
  23.1 0.0 copy-start
  23.1 0.0 copy-start.1
  23.2 0.0 copy-start.2
  23.2 0.0 copy-start.3
  23.2 0.0 copy-start.4
  23.2 0.0 copy-start.5
  23.2 0.0 copy-start.6
  23.2 0.0 copy-start.7
  23.2 11.0 %edges.1 = (bf16[768,512]{1,0:T(8,128)(2,1)S(1)}, bf16[2,768,256]{2,1,0:T(8,128)(2,1)S(1)}, bf16[4096,512]{1,0:T(8,128)(2,1)S(1)}) custom-call(s32[32,128]{1,0:T(8,128)S(1)} %get-tuple-element.26.slot_s.slots, s32[32,128]{1,0:T(8,128)S(1)} %get-tuple-element.26.slot_s.slots, s32[4096,128]{1,0:T(8,128)S(1)} %get-tuple-element.27.slot_col, ...), custom_call_target="tpu_custom_call" | custom-call | tf_op jit(solution)/shard_map/edges/pallas_call | solution.py:541
  34.3 0.0 copy-done
  34.3 0.0 copy-done.1
  34.3 0.0 copy-done.2
  34.3 0.0 copy-done.3
  34.3 0.0 copy-done.4
  34.3 0.0 copy-done.5
  34.3 0.0 copy-done.6
  34.3 0.0 copy-done.7
  34.3 73.3 %back.1 = (bf16[320,512]{1,0:T(8,128)(2,1)S(1)}, bf16[320,512]{1,0:T(8,128)(2,1)S(1)}, bf16[8,64,512]{2,1,0:T(8,128)(2,1)S(1)}, bf16[8,64,256]{2,1,0:T(8,128)(2,...) custom-call(bf16[768,384]{1,0:T(8,128)(2,1)S(1)} %get-tuple-element.24.p, ...), custom_call_target="tpu_custom_call" | custom-call | tf_op jit(solution)/shard_map/back/pallas_call | solution.py:572
  107.7 2.1 %write.1 = (bf16[320,512]{1,0:T(8,128)(2,1)}, bf16[320,512]{1,0:T(8,128)(2,1)}, f32[512,512]{1,0:T(8,128)}, f32[512,512]{1,0:T(8,128)}, f32[512,512]{1,0:T(8,128)}) custom-call(bf16[320,512]{1,0:T(8,128)(2,1)S(1)} %get-tuple-element.36.mo, bf16[320,512]{1,0:T(8,128)(2,1)S(1)} %get-tuple-element.37.gm, bf16[512,512]{1,0:T(8,128)(2,1)S(1)} %bitcast.16, ...), custom_call_target="tpu_custom_call" | custom-call | tf_op jit(solution)/shard_map/write/pallas_call | solution.py:591
Async XLA Ops:
  23.1 11.1 %copy-start = (bf16[512,512]{1,0:T(8,128)(2,1)S(1)}, bf16[512,512]{1,0:T(8,128)(2,1)}, u32[]{:S(2)}) copy-start(bf16[512,512]{1,0:T(8,128)(2,1)} %u_mesh.1) | copy-start | bytes 1572868
  23.1 11.1 %copy-start.1 = (bf16[320,512]{1,0:T(8,128)(2,1)S(1)}, bf16[320,512]{1,0:T(8,128)(2,1)}, u32[]{:S(2)}) copy-start(bf16[320,512]{1,0:T(8,128)(2,1)} %ml.1) | copy-start | bytes 983044
  23.2 11.1 %copy-start.2 = (bf16[512,512]{1,0:T(8,128)(2,1)S(1)}, bf16[512,512]{1,0:T(8,128)(2,1)}, u32[]{:S(2)}) copy-start(bf16[512,512]{1,0:T(8,128)(2,1)} %w_edge.1) | copy-start | bytes 1572868
  23.2 11.1 %copy-start.3 = (bf16[512,512]{1,0:T(8,128)(2,1)S(1)}, bf16[512,512]{1,0:T(8,128)(2,1)}, u32[]{:S(2)}) copy-start(bf16[512,512]{1,0:T(8,128)(2,1)} %w_self.1) | copy-start | bytes 1572868
  23.2 11.1 %copy-start.4 = (bf16[512,512]{1,0:T(8,128)(2,1)S(1)}, bf16[512,512]{1,0:T(8,128)(2,1)}, u32[]{:S(2)}) copy-start(bf16[512,512]{1,0:T(8,128)(2,1)} %w_agg.1) | copy-start | bytes 1572868
  23.2 11.1 %copy-start.5 = (bf16[512,512]{1,0:T(8,128)(2,1)S(1)}, bf16[512,512]{1,0:T(8,128)(2,1)}, u32[]{:S(2)}) copy-start(bf16[512,512]{1,0:T(8,128)(2,1)} %w_node.1) | copy-start | bytes 1572868
  23.2 11.1 %copy-start.6 = (bf16[320,512]{1,0:T(8,128)(2,1)S(1)}, bf16[320,512]{1,0:T(8,128)(2,1)}, u32[]{:S(2)}) copy-start(bf16[320,512]{1,0:T(8,128)(2,1)} %ct.1) | copy-start | bytes 983044
  23.2 11.1 %copy-start.7 = (f32[512]{0:T(512)S(1)}, f32[512]{0:T(512)}, u32[]{:S(2)}) copy-start(f32[512]{0:T(512)} %param.32) | copy-start | bytes 6148

commit v5 on v4

--- a/solution.py
+++ b/solution.py
@@ -274,10 +274,22 @@
         s_out[c] = acc[:, width + c * half : width + (c + 1) * half].astype(BF16)
 
 
-def make_sum(axes, scale, big, small, width, all1, in1, mid, in2, all2, q1, q2, q3, q4):
-    n, m = axes[big], axes[small]
+def make_sum(nb, nm, scale, out, landed, tot, in1, mid, in2, qp, q1, q2, q3, q4):
     rows = in1.shape[1]
+    me = lax.axis_index("mesh")
+    band = lax.axis_index("band")
+    core = lax.rem(band, 2)
+    place = band // 2
+    across = nb // 2
+    partner = {"band": band + 1 - 2 * core}
     live = {}
+
+    def remote(src, dst, send, recv, device):
+        copy = pltpu.make_async_remote_copy(
+            src_ref=src, dst_ref=dst, send_sem=send, recv_sem=recv, device_id=device, device_id_type=MESH
+        )
+        copy.start()
+        return copy
 
     def add(ref, count):
         total = ref[0].astype(F32)
@@ -286,62 +298,45 @@
         return total
 
     def start(src):
-        def part(p):
-            return src.at[pl.ds(pl.multiple_of(p * rows, 16), rows), :]
-
-        live[1] = send_all(big, n, part, lambda q: in1.at[q], q1.at[0], q1.at[1])
-        me = lax.axis_index(big)
-        in1[me] = src[pl.ds(pl.multiple_of(me * rows, 16), rows), :]
-
-    def spread_big(values):
-        me = lax.axis_index(big)
-        all1[me] = values.astype(BF16)
-        live[4] = send_all(big, n, lambda p: all1.at[me], lambda q: all1.at[q], q4.at[0], q4.at[1])
+        live[0] = src
+        live[1] = remote(src.at[1 - core], landed, qp.at[0], qp.at[1], partner)
+
+    def scatter():
+        live[1].wait()
+        tot[...] = (live[0][core].astype(F32) + landed[...].astype(F32)).astype(BF16)
+        live[2] = send_all(
+            "mesh", nm, lambda p: tot.at[pl.ds(pl.multiple_of(p * rows, 16), rows), :],
+            lambda q: in1.at[q], q1.at[0], q1.at[1])
+        in1[me] = tot[pl.ds(pl.multiple_of(me * rows, 16), rows), :]
+
+    def middle():
+        wait_all(live[2])
+        mid[...] = add(in1, nm).astype(BF16)
+        live[3] = [
+            remote(mid, in2.at[place], q2.at[0, d], q2.at[1, d],
+                   {"band": lax.rem(place + d, across) * 2 + core})
+            for d in range(1, across)
+        ]
+        in2[place] = mid[...]
+
+    def gather():
+        wait_all(live[3])
+        out[core, me] = (add(in2, across) * scale).astype(BF16)
+        live[4] = send_all("mesh", nm, lambda p: out.at[core, me], lambda q: out.at[core, q], q3.at[0], q3.at[1])
+        live[5] = [remote(out.at[core, me], out.at[core, me], q4.at[0, 0], q4.at[1, 0], partner)]
+
+    def forward():
+        for d, copy in enumerate(live[4], 1):
+            copy.wait_recv()
+            part = out.at[core, lax.rem(me + nm - d, nm)]
+            live[5].append(remote(part, part, q4.at[0, d], q4.at[1, d], partner))
 
     def finish():
-        wait_all(live[4])
-
-    if small == "band":
-
-        def middle():
-            wait_all(live[1])
-            mid[...] = add(in1, n).astype(BF16)
-            live[2] = send_all(small, m, lambda p: mid, lambda q: in2.at[q], q2.at[0], q2.at[1])
-            in2[lax.axis_index(small)] = mid[...]
-
-        def gather():
-            wait_all(live[2])
-            spread_big(add(in2, m) * scale)
-
-        return start, middle, gather, None, finish
-
-    pr, pc = mid.shape[1], mid.shape[2]
-    cols = width // pc
-
-    def middle():
-        wait_all(live[1])
-        total = add(in1, n)
-        for i in range(m):
-            a, c = i // cols, i % cols
-            mid[i] = total[a * pr : (a + 1) * pr, c * pc : (c + 1) * pc]
-        live[2] = send_all(small, m, lambda p: mid.at[p], lambda q: in2.at[q], q2.at[0], q2.at[1])
-        me = lax.axis_index(small)
-        in2[me] = mid[me]
-
-    def gather():
-        wait_all(live[2])
-        me = lax.axis_index(small)
-        all2[me] = add(in2, m) * scale
-        live[3] = send_all(small, m, lambda p: all2.at[me], lambda q: all2.at[q], q3.at[0], q3.at[1])
-
-    def spread():
-        wait_all(live[3])
-        spread_big(jnp.concatenate(
-            [jnp.concatenate([all2[a * cols + c] for c in range(cols)], axis=1) for a in range(m // cols)],
-            axis=0,
-        ))
-
-    return start, middle, gather, spread, finish
+        for copy in live[4]:
+            copy.wait_send()
+        wait_all(live[5])
+
+    return start, scatter, middle, gather, forward, finish
 
 
 GB = 1024
@@ -350,8 +345,8 @@
 def back_kernel(
     nb, nm, scale, pick, ml, ct, b_node, grid_rows, a_part, s_part, w_edge, w_self, w_agg,
     w_node, u_mesh, slot_col, slope, latent_t, rows_in,
-    mesh_out, grad_mesh, oe, ou0, ou1, og0, og1,
-    a_in, s_in, asked, landed, hot_s, lat_e, rows_t, acc, ge, gg, gu,
+    mesh_out, grad_mesh, oe, o0, o1,
+    a_in, s_in, asked, landed, hot_s, lat_e, rows_t, acc, ge, g2,
     sa, ra, ss, rs, sh, rh, *sums,
 ):
     mesh_dev, width = ml.shape
@@ -361,14 +356,9 @@
     grid_dev = latent_t.shape[1]
     flat = nm * CAP
     me = lax.axis_index("mesh")
-    axes = {"band": nb, "mesh": nm}
-    sum_e, sum_u0, sum_u1, sum_g0, sum_g1 = [
-        make_sum(axes, scale, big, small, w, (oe, ou0, ou1, og0, og1)[i], *sums[i * 8 : (i + 1) * 8])
-        for i, (big, small, w) in enumerate(
-            (("band", "mesh", width),) + (("band", "mesh", half),) * 2 + (("mesh", "band", half),) * 2
-        )
+    sum_e, sum_0, sum_1 = [
+        make_sum(nb, nm, scale, out, *sums[i * 10 : (i + 1) * 10]) for i, out in enumerate((oe, o0, o1))
     ]
-    sum_u, sum_g = (sum_u0, sum_u1), (sum_g0, sum_g1)
 
     def send_slopes(c):
         s_in[c, me] = s_part[c, me]
@@ -417,7 +407,9 @@
                                sh.at[c], rh.at[c]))
         landed[c, me] = asked[c, me]
     sent_s.append(send_slopes(1))
-    ge[...] = dot_tn(acts, g_agg).astype(BF16)
+    g_edge = dot_tn(acts, g_agg).astype(BF16)
+    ge[0] = g_edge[:, 0:half]
+    ge[1] = g_edge[:, half:]
     sum_e[0](ge)
     mesh_out[...] = (ml[...].astype(F32) + dot(node_act.astype(BF16), w_node[...])).astype(BF16)
     part = ct[...].astype(F32) + dot_nt(g_node, w_self[...])
@@ -428,54 +420,52 @@
         wait_all(sent_h[c])
         table = landed[c].reshape(flat, half)
         pm = (table.astype(F32) * s_part[c].reshape(flat, half).astype(F32)).astype(BF16)
-        gu[c] = dot(rows_t[...], pm).astype(BF16)
-        sum_u[c][0](gu.at[c])
+        g2[c, 1] = dot(rows_t[...], pm).astype(BF16)
         for b in range(rows * 128 // GB):
             cut = slice(b * GB, (b + 1) * GB)
             g = (dot(hot_s[cut, :], table) * slope[cut, col].astype(F32)).astype(BF16)
             acc[...] += dot(lat_e[:, cut], g)
             if b in between:
                 between[b]()
-        gg[c] = acc[...].astype(BF16)
-        sum_g[c][0](gg.at[c])
+        g2[c, 0] = acc[...].astype(BF16)
 
     last = rows * 128 // GB - 1
-    halves(0, {min(1, last): sum_e[1]})
-    halves(1, {0: sum_u0[1]})
-    sum_e[2]()
-    sum_u1[1]()
-    sum_u0[2]()
-    sum_g0[1]()
+    sum_e[1]()
+    halves(0, {})
+    sum_0[0](g2.at[0])
+    halves(1, {min(1, last): sum_0[1]})
+    sum_1[0](g2.at[1])
     wait_all(sent_s[0])
     wait_all(sent_s[1])
     slopes = jnp.concatenate(
         [dot_tn(pick[...], s_in[c].reshape(flat, half))[0:mesh_dev] for c in range(2)], axis=1
     )
+    sum_1[1]()
+    sum_e[2]()
     g_pmesh = (h * slopes).astype(BF16)
     grad_mesh[...] = (part + dot_nt(g_pmesh, u_mesh[...])).astype(BF16)
     sum_e[3]()
-    sum_g0[2]()
-    sum_u0[3]()
-    sum_g1[1]()
-    sum_u1[2]()
-    sum_g1[2]()
-    sum_u1[3]()
+    sum_0[2]()
+    sum_0[3]()
+    sum_1[2]()
+    sum_1[3]()
     sum_e[4]()
-    sum_g0[4]()
-    sum_u0[4]()
-    sum_u1[4]()
-    sum_g1[4]()
-
-
-def write_kernel(mo, gm, e, u0, u1, g0, g1, mo_out, gm_out, e_out, g_out, u_out):
-    half = g0.shape[1]
+    sum_0[4]()
+    sum_1[4]()
+    sum_e[5]()
+    sum_0[5]()
+    sum_1[5]()
+
+
+def write_kernel(mo, gm, e, g0, g1, mo_out, gm_out, e_out, g_out, u_out):
+    half = e.shape[2]
     mo_out[...] = mo[...]
     gm_out[...] = gm[...]
-    e_out[...] = e[...].astype(F32)
-    u_out[:, 0:half] = u0[...].astype(F32)
-    u_out[:, half:] = u1[...].astype(F32)
-    g_out[:, 0:half] = g0[...].astype(F32)
-    g_out[:, half:] = g1[...].astype(F32)
+    for c, both in enumerate((g0, g1)):
+        col = slice(c * half, (c + 1) * half)
+        e_out[:, col] = e[c].astype(F32)
+        g_out[:, col] = both[0].astype(F32)
+        u_out[:, col] = both[1].astype(F32)
 
 
 def vmem():
@@ -552,34 +542,26 @@
         compiler_params=params(16),
         name="edges",
     )(slots, slots, slot_col, table, pre_grid, bias)
-    sums = []
-    for n, m, w in ((nb, nm, width), (nb, nm, half), (nb, nm, half), (nm, nb, half), (nm, nb, half)):
-        big = width // n
-        if n == nm:
-            mid = [pltpu.VMEM((big, w), BF16), pltpu.VMEM((m, big, w), BF16), pltpu.VMEM((8, 128), F32)]
-        else:
-            across = min(m, w // 128)
-            piece = pltpu.VMEM((m, big // (m // across), w // across), F32)
-            mid = [piece] * 3
-        sums += [pltpu.VMEM((n, big, w), BF16)] + mid + [
-            sem((2, n)), sem((2, m)), sem((2, m)), sem((2, n)),
-        ]
+    part = width // nm
+    sums = [
+        pltpu.VMEM((width, half), BF16), pltpu.VMEM((width, half), BF16), pltpu.VMEM((nm, part, half), BF16),
+        pltpu.VMEM((part, half), BF16), pltpu.VMEM((nb // 2, part, half), BF16),
+        sem((2,)), sem((2, nm)), sem((2, nb)), sem((2, nm)), sem((2, nm)),
+    ] * 3
     scale = (edges * nb * nm) ** (-0.5)
     node = shape((mesh_dev, width), BF16)
-    slim_u = shape((nb, width // nb, half), BF16)
-    slim_g = shape((nm, width // nm, half), BF16)
+    summed = shape((2, nm, part, half), BF16)
     blocks = pltpu.VMEM((2, nm, CAP, half), BF16)
     outs = pl.pallas_call(
         functools.partial(back_kernel, nb, nm, scale),
-        out_shape=(node, node, shape((nb, width // nb, width), BF16), slim_u, slim_u, slim_g, slim_g),
+        out_shape=(node, node, summed, summed, summed),
         in_specs=[vmem()] * 16,
-        out_specs=(vmem(),) * 7,
+        out_specs=(vmem(),) * 5,
         scratch_shapes=[
             pltpu.VMEM((nm, CAP, width), BF16), blocks, blocks, blocks,
             pltpu.VMEM((edges, slots_n), BF16), pltpu.VMEM((width, edges), BF16),
             pltpu.VMEM((width, slots_n), BF16), pltpu.VMEM((width, half), F32),
-            pltpu.VMEM((width, width), BF16), pltpu.VMEM((2, width, half), BF16),
-            pltpu.VMEM((2, width, half), BF16),
+            pltpu.VMEM((2, width, half), BF16), pltpu.VMEM((2, 2, width, half), BF16),
             sem((nm,)), sem((nm,)), sem((2, nm)), sem((2, nm)), sem((2, nm)), sem((2, nm)),
         ] + sums,
         compiler_params=params(38, 1),
@@ -591,11 +573,11 @@
     return pl.pallas_call(
         write_kernel,
         out_shape=(node, node, final, final, final),
-        in_specs=[vmem()] * 7,
+        in_specs=[vmem()] * 5,
         out_specs=(vmem(),) * 5,
         compiler_params=params(16),
         name="write",
-    )(*outs[:2], *[o.reshape(width, o.shape[2]) for o in outs[2:]])
+    )(*outs[:2], *[o.reshape(2, width, half) for o in outs[2:]])
 
 
 def solution(mesh):

time: 110 us -> 102 us (0.927)
  Pallas kernels: 109 us -> 101 us
    pallas_call x1, Pallas kernels: 73.3 us -> 65.2 us  [shards(): pl.pallas_call(functools.partial(back_kernel, nb, nm, scale), out_shape=(...]
where the time goes in v5:
time: 102 us
  Pallas kernels  101 us (99%)
    pallas_call x1, Pallas kernels, shards(): pl.pallas_call(functools.partial(back_kernel, nb, nm, scale), out_shape=(...  65.2 us
    pallas_call x1, Pallas kernels, shards(): pl.pallas_call(functools.partial(fetch_kernel, nb, nm), out_shape=(shape(...  22.5 us
    pallas_call x1, Pallas kernels, shards(): pl.pallas_call(edge_kernel, out_shape=(shape((slots_n, width), BF16), sha...  11 us
    pallas_call x1, Pallas kernels, shards(): pl.pallas_call(write_kernel, out_shape=(node, node, final, final, final),...  2.09 us

profile of v5, /device:TPU:1, one launch (start us, length us, event | category | flops | bytes accessed | tf_op | source)
XLA Modules:
  0.0 101.7 jit_solution(11421995856245491695)
XLA Ops:
  0.6 22.5 %fetch.1 = (bf16[768,512]{1,0:T(8,128)(2,1)S(1)}, bf16[768,512]{1,0:T(8,128)(2,1)S(1)}, bf16[768,384]{1,0:T(8,128)(2,1)S(1)}, bf16[512,1024]{1,0:T(8,128)(2,1)S(...) custom-call(s32[32,128]{1,0:T(8,128)} %bitcast.19, ...), custom_call_target="tpu_custom_call" | custom-call | tf_op jit(solution)/shard_map/fetch/pallas_call | solution.py:500
  23.1 0.0 copy-start
  23.1 0.0 copy-start.1
  23.2 0.0 copy-start.2
  23.2 0.0 copy-start.3
  23.2 0.0 copy-start.4
  23.2 0.0 copy-start.5
  23.2 0.0 copy-start.6
  23.2 0.0 copy-start.7
  23.2 11.0 %edges.1 = (bf16[768,512]{1,0:T(8,128)(2,1)S(1)}, bf16[2,768,256]{2,1,0:T(8,128)(2,1)S(1)}, bf16[4096,512]{1,0:T(8,128)(2,1)S(1)}) custom-call(s32[32,128]{1,0:T(8,128)S(1)} %get-tuple-element.24.slot_s.slots, s32[32,128]{1,0:T(8,128)S(1)} %get-tuple-element.24.slot_s.slots, s32[4096,128]{1,0:T(8,128)S(1)} %get-tuple-element.25.slot_col, ...), custom_call_target="tpu_custom_call" | custom-call | tf_op jit(solution)/shard_map/edges/pallas_call | solution.py:531
  34.3 0.0 copy-done
  34.3 0.0 copy-done.1
  34.3 0.0 copy-done.2
  34.3 0.0 copy-done.3
  34.3 0.0 copy-done.4
  34.3 0.0 copy-done.5
  34.3 0.0 copy-done.6
  34.3 0.0 copy-done.7
  34.3 65.2 %back.1 = (bf16[320,512]{1,0:T(8,128)(2,1)S(1)}, bf16[320,512]{1,0:T(8,128)(2,1)S(1)}, bf16[2,16,32,256]{3,2,1,0:T(8,128)(2,1)S(1)}, bf16[2,16,32,256]{3,2,1,0:T(8,128)(2,1)S(1)}, bf16[2,16,32,256]{3,2,1,0:T(8,128)(2,1)S(1)}) custom-call(bf16[768,384]{1,0:T(8,128)(2,1)S(1)} %get-tuple-element.22.pick, bf16[320,512]{1,0:T(8,128)(2,1)S(1)} %copy-done.1, ...), custom_call_target="tpu_custom_call" | custom-call | tf_op jit(solution)/shard_map/back/pallas_call | solution.py:555
  99.6 2.1 %write.1 = (bf16[320,512]{1,0:T(8,128)(2,1)}, bf16[320,512]{1,0:T(8,128)(2,1)}, f32[512,512]{1,0:T(8,128)}, f32[512,512]{1,0:T(8,128)}, f32[512,512]{1,0:T(8,128)}) custom-call(bf16[320,512]{1,0:T(8,128)(2,1)S(1)} %get-tuple-element.34.mo, bf16[320,512]{1,0:T(8,128)(2,1)S(1)} %get-tuple-element.35.gm, bf16[2,512,256]{2,1,0:T(8,128)(2,1)S(1)} %bitcast.14, ...), custom_call_target="tpu_custom_call" | custom-call | tf_op jit(solution)/shard_map/write/pallas_call | solution.py:573
Async XLA Ops:
  23.1 11.1 %copy-start = (bf16[512,512]{1,0:T(8,128)(2,1)S(1)}, bf16[512,512]{1,0:T(8,128)(2,1)}, u32[]{:S(2)}) copy-start(bf16[512,512]{1,0:T(8,128)(2,1)} %u_mesh.1) | copy-start | bytes 1572868
  23.1 11.1 %copy-start.1 = (bf16[320,512]{1,0:T(8,128)(2,1)S(1)}, bf16[320,512]{1,0:T(8,128)(2,1)}, u32[]{:S(2)}) copy-start(bf16[320,512]{1,0:T(8,128)(2,1)} %ml.1) | copy-start | bytes 983044
  23.2 11.1 %copy-start.2 = (bf16[512,512]{1,0:T(8,128)(2,1)S(1)}, bf16[512,512]{1,0:T(8,128)(2,1)}, u32[]{:S(2)}) copy-start(bf16[512,512]{1,0:T(8,128)(2,1)} %w_edge.1) | copy-start | bytes 1572868
  23.2 11.1 %copy-start.3 = (bf16[512,512]{1,0:T(8,128)(2,1)S(1)}, bf16[512,512]{1,0:T(8,128)(2,1)}, u32[]{:S(2)}) copy-start(bf16[512,512]{1,0:T(8,128)(2,1)} %w_self.1) | copy-start | bytes 1572868
  23.2 11.1 %copy-start.4 = (bf16[512,512]{1,0:T(8,128)(2,1)S(1)}, bf16[512,512]{1,0:T(8,128)(2,1)}, u32[]{:S(2)}) copy-start(bf16[512,512]{1,0:T(8,128)(2,1)} %w_agg.1) | copy-start | bytes 1572868
  23.2 11.1 %copy-start.5 = (bf16[512,512]{1,0:T(8,128)(2,1)S(1)}, bf16[512,512]{1,0:T(8,128)(2,1)}, u32[]{:S(2)}) copy-start(bf16[512,512]{1,0:T(8,128)(2,1)} %w_node.1) | copy-start | bytes 1572868
  23.2 11.1 %copy-start.6 = (bf16[320,512]{1,0:T(8,128)(2,1)S(1)}, bf16[320,512]{1,0:T(8,128)(2,1)}, u32[]{:S(2)}) copy-start(bf16[320,512]{1,0:T(8,128)(2,1)} %ct.1) | copy-start | bytes 983044
  23.2 11.1 %copy-start.7 = (f32[512]{0:T(512)S(1)}, f32[512]{0:T(512)}, u32[]{:S(2)}) copy-start(f32[512]{0:T(512)} %param.32) | copy-start | bytes 6148

commit v6 on v5

--- a/solution.py
+++ b/solution.py
@@ -441,12 +441,12 @@
         [dot_tn(pick[...], s_in[c].reshape(flat, half))[0:mesh_dev] for c in range(2)], axis=1
     )
     sum_1[1]()
+    sum_0[2]()
     sum_e[2]()
     g_pmesh = (h * slopes).astype(BF16)
     grad_mesh[...] = (part + dot_nt(g_pmesh, u_mesh[...])).astype(BF16)
+    sum_0[3]()
     sum_e[3]()
-    sum_0[2]()
-    sum_0[3]()
     sum_1[2]()
     sum_1[3]()
     sum_e[4]()

time: 102 us -> 102 us (level)
  no operation moved by 1% of the time
where the time goes in v6:
time: 102 us
  Pallas kernels  101 us (99%)
    pallas_call x1, Pallas kernels, shards(): pl.pallas_call(functools.partial(back_kernel, nb, nm, scale), out_shape=(...  65.3 us
    pallas_call x1, Pallas kernels, shards(): pl.pallas_call(functools.partial(fetch_kernel, nb, nm), out_shape=(shape(...  22.5 us
    pallas_call x1, Pallas kernels, shards(): pl.pallas_call(edge_kernel, out_shape=(shape((slots_n, width), BF16), sha...  11 us
    pallas_call x1, Pallas kernels, shards(): pl.pallas_call(write_kernel, out_shape=(node, node, final, final, final),...  2.09 us

profile of v6, /device:TPU:1, one launch (start us, length us, event | category | flops | bytes accessed | tf_op | source)
XLA Modules:
  0.0 101.8 jit_solution(13877686425903156713)
XLA Ops:
  0.6 22.5 %fetch.1 = (bf16[768,512]{1,0:T(8,128)(2,1)S(1)}, bf16[768,512]{1,0:T(8,128)(2,1)S(1)}, bf16[768,384]{1,0:T(8,128)(2,1)S(1)}, bf16[512,1024]{1,0:T(8,128)(2,1)S(...) custom-call(s32[32,128]{1,0:T(8,128)} %bitcast.19, ...), custom_call_target="tpu_custom_call" | custom-call | tf_op jit(solution)/shard_map/fetch/pallas_call | solution.py:500
  23.1 0.0 copy-start
  23.1 0.0 copy-start.1
  23.2 0.0 copy-start.2
  23.2 0.0 copy-start.3
  23.2 0.0 copy-start.4
  23.2 0.0 copy-start.5
  23.2 0.0 copy-start.6
  23.2 0.0 copy-start.7
  23.2 11.0 %edges.1 = (bf16[768,512]{1,0:T(8,128)(2,1)S(1)}, bf16[2,768,256]{2,1,0:T(8,128)(2,1)S(1)}, bf16[4096,512]{1,0:T(8,128)(2,1)S(1)}) custom-call(s32[32,128]{1,0:T(8,128)S(1)} %get-tuple-element.24.slot_s.slots, s32[32,128]{1,0:T(8,128)S(1)} %get-tuple-element.24.slot_s.slots, s32[4096,128]{1,0:T(8,128)S(1)} %get-tuple-element.25.slot_col, ...), custom_call_target="tpu_custom_call" | custom-call | tf_op jit(solution)/shard_map/edges/pallas_call | solution.py:531
  34.3 0.0 copy-done
  34.3 0.0 copy-done.1
  34.3 0.0 copy-done.2
  34.3 0.0 copy-done.3
  34.3 0.0 copy-done.4
  34.3 0.0 copy-done.5
  34.3 0.0 copy-done.6
  34.3 0.0 copy-done.7
  34.3 65.3 %back.1 = (bf16[320,512]{1,0:T(8,128)(2,1)S(1)}, bf16[320,512]{1,0:T(8,128)(2,1)S(1)}, bf16[2,16,32,256]{3,2,1,0:T(8,128)(2,1)S(1)}, bf16[2,16,32,256]{3,2,1,0:T(8,128)(2,1)S(1)}, bf16[2,16,32,256]{3,2,1,0:T(8,128)(2,1)S(1)}) custom-call(bf16[768,384]{1,0:T(8,128)(2,1)S(1)} %get-tuple-element.22.pick, bf16[320,512]{1,0:T(8,128)(2,1)S(1)} %copy-done.1, ...), custom_call_target="tpu_custom_call" | custom-call | tf_op jit(solution)/shard_map/back/pallas_call | solution.py:555
  99.7 2.1 %write.1 = (bf16[320,512]{1,0:T(8,128)(2,1)}, bf16[320,512]{1,0:T(8,128)(2,1)}, f32[512,512]{1,0:T(8,128)}, f32[512,512]{1,0:T(8,128)}, f32[512,512]{1,0:T(8,128)}) custom-call(bf16[320,512]{1,0:T(8,128)(2,1)S(1)} %get-tuple-element.34.mo, bf16[320,512]{1,0:T(8,128)(2,1)S(1)} %get-tuple-element.35.gm, bf16[2,512,256]{2,1,0:T(8,128)(2,1)S(1)} %bitcast.14, ...), custom_call_target="tpu_custom_call" | custom-call | tf_op jit(solution)/shard_map/write/pallas_call | solution.py:573
Async XLA Ops:
  23.1 11.1 %copy-start = (bf16[512,512]{1,0:T(8,128)(2,1)S(1)}, bf16[512,512]{1,0:T(8,128)(2,1)}, u32[]{:S(2)}) copy-start(bf16[512,512]{1,0:T(8,128)(2,1)} %u_mesh.1) | copy-start | bytes 1572868
  23.1 11.1 %copy-start.1 = (bf16[320,512]{1,0:T(8,128)(2,1)S(1)}, bf16[320,512]{1,0:T(8,128)(2,1)}, u32[]{:S(2)}) copy-start(bf16[320,512]{1,0:T(8,128)(2,1)} %ml.1) | copy-start | bytes 983044
  23.2 11.1 %copy-start.2 = (bf16[512,512]{1,0:T(8,128)(2,1)S(1)}, bf16[512,512]{1,0:T(8,128)(2,1)}, u32[]{:S(2)}) copy-start(bf16[512,512]{1,0:T(8,128)(2,1)} %w_edge.1) | copy-start | bytes 1572868
  23.2 11.1 %copy-start.3 = (bf16[512,512]{1,0:T(8,128)(2,1)S(1)}, bf16[512,512]{1,0:T(8,128)(2,1)}, u32[]{:S(2)}) copy-start(bf16[512,512]{1,0:T(8,128)(2,1)} %w_self.1) | copy-start | bytes 1572868
  23.2 11.1 %copy-start.4 = (bf16[512,512]{1,0:T(8,128)(2,1)S(1)}, bf16[512,512]{1,0:T(8,128)(2,1)}, u32[]{:S(2)}) copy-start(bf16[512,512]{1,0:T(8,128)(2,1)} %w_agg.1) | copy-start | bytes 1572868
  23.2 11.1 %copy-start.5 = (bf16[512,512]{1,0:T(8,128)(2,1)S(1)}, bf16[512,512]{1,0:T(8,128)(2,1)}, u32[]{:S(2)}) copy-start(bf16[512,512]{1,0:T(8,128)(2,1)} %w_node.1) | copy-start | bytes 1572868
  23.2 11.1 %copy-start.6 = (bf16[320,512]{1,0:T(8,128)(2,1)S(1)}, bf16[320,512]{1,0:T(8,128)(2,1)}, u32[]{:S(2)}) copy-start(bf16[320,512]{1,0:T(8,128)(2,1)} %ct.1) | copy-start | bytes 983044
  23.2 11.1 %copy-start.7 = (f32[512]{0:T(512)S(1)}, f32[512]{0:T(512)}, u32[]{:S(2)}) copy-start(f32[512]{0:T(512)} %param.32) | copy-start | bytes 6148
